TPU v7x, 32 devices: a whole 2x2x4 slice. The times are simulated.
32 devices in a mesh: node: 2 (over y), gz: 16 (over z, x, core).
Axes of the slice: x: 2, y: 2, z: 4, core: 2. Of those that a mesh axis runs over, the one named last changes fastest.
Arguments:
- source: float32 [2, 64, 512, 256], P(None, ('node', 'gz')), parts along dimension 1, may hold values from -56 to 56
- layer_ids: int32 [64, 256], P(('node', 'gz')), parts along dimension 0, may hold values from 0 to 15
- conduct_table: float32 [16], replicated, may hold values from 0.35 to 3.75
- shift: float32 [4], P('node'), parts along dimension 0, may hold values from 0.2 to 1
Outputs:
- solution_field: float32 [2, 64, 512, 256], P(None, ('node', 'gz')), parts along dimension 1
- residual_norms: float32 [4], P('node'), parts along dimension 0
There are 2 independent parts, one for each index of `node`. A program takes and returns all parts, laid end to end along the dimension named above; an argument that names none is the same for every part. Nothing has to cross between parts.
All inputs are finite; a program needn't handle non-finite values.
Results may differ from a plain program's by a relative error of at most 0.0003.
Values sent between devices are 32-bit elements; how exact they have to be, the bound alone decides.
A program may use at most 64 MiB of HBM per device.

v0:
```python
import functools

import jax
import jax.numpy as jnp
import numpy as np
from jax import lax
from jax.experimental import pallas as pl
from jax.experimental.pallas import tpu as pltpu
from jax.sharding import PartitionSpec as P

ITERS = 2


relax = 0.6
highest = lax.Precision.HIGH


def with_halo(cells, sides, width):
    for axis, dim in sides:
        count = lax.axis_size(axis)
        ends = count - 1
        head = lax.slice_in_dim(cells, 0, width, axis=dim)
        tail = lax.slice_in_dim(cells, cells.shape[dim] - width, cells.shape[dim], axis=dim)
        cells = jnp.concatenate(
            [
                lax.ppermute(tail, axis, [(i, (i + 1) % count) for i in range(ends)]),
                cells,
                lax.ppermute(head, axis, [((i + 1) % count, i) for i in range(ends)]),
            ],
            axis=dim,
        )
    return cells


def sine_table(length):
    indices = lax.iota(jnp.int32, length) + 1
    product = indices[:, None] * indices[None, :] % (2 * (length + 1))
    return jnp.sqrt(2.0 / (length + 1)) * jnp.sin(
        jnp.pi / (length + 1) * product.astype(jnp.float32)
    )


def sine_eigen(length):
    indices = lax.iota(jnp.float32, length) + 1.0
    return 2.0 - 2.0 * jnp.cos(jnp.pi / (length + 1) * indices)


def dft_tables(length):
    indices = lax.iota(jnp.int32, length)
    product = indices[:, None] * indices[None, :] % length
    angles = 2.0 * jnp.pi / length * product.astype(jnp.float32)
    return (jnp.cos(angles), jnp.sin(angles))


def transform(field, cos_t, sin_t, inverse):

    def project(component, matrix):
        return jnp.einsum("zxy,xk->zky", component, matrix, precision=highest)

    re_cos = project(field[0], cos_t)
    re_sin = project(field[0], sin_t)
    im_cos = project(field[1], cos_t)
    im_sin = project(field[1], sin_t)
    if inverse:
        return jnp.stack([re_cos - im_sin, im_cos + re_sin]) / cos_t.shape[0]
    return jnp.stack([re_cos + im_sin, im_cos - re_sin])


def expand(weights):
    return weights[None, :, None, :]


def yz_part(field, upper, lower, conduct, cond_hi, cond_lo):
    cond_pad = jnp.pad(conduct, ((0, 0), (1, 1)), mode="edge")
    face_yp = 0.5 * (conduct + cond_pad[:, 2:])
    face_ym = 0.5 * (conduct + cond_pad[:, :-2])
    face_zp = 0.5 * (conduct + cond_hi)
    face_zm = 0.5 * (conduct + cond_lo)
    field_pad = jnp.pad(field, ((0, 0), (0, 0), (0, 0), (1, 1)))
    total = expand(face_yp) * (field - field_pad[..., 2:]) + expand(face_ym) * (
        field - field_pad[..., :-2]
    )
    return total + expand(face_zp) * (field - upper) + expand(face_zm) * (field - lower)


def shift_mult(shift_re, shift_im, field):
    return jnp.stack(
        [shift_re * field[0] - shift_im * field[1], shift_re * field[1] + shift_im * field[0]]
    )


def sine_both(field, sine_y, sine_z):
    field = jnp.einsum("pzxy,yj->pzxj", field, sine_y, precision=highest)
    return jnp.einsum("pzxy,zk->pkxy", field, sine_z, precision=highest)


def precondition(coeffs, mode_eig, mean_cond, shift_re, shift_im, sine_y, sine_z, eig_y, eig_z):
    coeffs = sine_both(coeffs, sine_y, sine_z)
    eigen = eig_z[:, None, None] + mode_eig[None, :, None] + eig_y[None, None, :]
    real_den = shift_re + mean_cond * eigen
    inv = 1.0 / (real_den * real_den + shift_im * shift_im)
    scaled = jnp.stack(
        [
            (coeffs[0] * real_den + coeffs[1] * shift_im) * inv,
            (coeffs[1] * real_den - coeffs[0] * shift_im) * inv,
        ]
    )
    return sine_both(scaled, sine_y, sine_z)


def body_plain(source, layer_ids, conduct_table, shift):
    shift_re = shift[0]
    shift_im = shift[1]
    planes = source.shape[1]
    length_x = source.shape[2]
    length_y = source.shape[3]
    groups = lax.axis_size("gz")
    length_z = planes * groups
    modes = length_x // groups
    first_mode = lax.axis_index("gz") * modes
    layers = conduct_table.shape[0]
    onehot = layer_ids[:, :, None] == lax.iota(jnp.int32, layers)[None, None, :]
    local = jnp.sum(jnp.where(onehot, conduct_table[None, None, :], 0.0), axis=-1)
    conduct = lax.all_gather(local, "gz", axis=0, tiled=True)
    mean_cond = jnp.sum(conduct) / (length_y * length_z)
    cond_z = jnp.pad(conduct, ((1, 1), (0, 0)), mode="edge")
    cos_t, sin_t = dft_tables(length_x)
    sine_y = sine_table(length_y)
    sine_z = sine_table(length_z)
    eig_y = sine_eigen(length_y)
    eig_z = sine_eigen(length_z)
    mode_ids = (first_mode + lax.iota(jnp.int32, modes)).astype(jnp.float32)
    mode_eig = 2.0 - 2.0 * jnp.cos(2.0 * jnp.pi / length_x * mode_ids)
    cells = length_x * length_y * length_z
    spectra = transform(source, cos_t, sin_t, False)
    forcing = lax.all_to_all(spectra, "gz", split_axis=2, concat_axis=1, tiled=True)
    partials = []
    solution = jnp.zeros_like(forcing)
    for iteration in range(ITERS):
        if iteration == 0:
            resid = forcing
        else:
            padded = jnp.pad(solution, ((0, 0), (1, 1), (0, 0), (0, 0)))
            lap = expand(conduct) * mode_eig[None, None, :, None] * solution
            lap = lap + yz_part(
                solution, padded[:, 2:], padded[:, :-2], conduct, cond_z[2:], cond_z[:-2]
            )
            resid = forcing - (shift_mult(shift_re, shift_im, solution) + lap)
        partials.append(jnp.sum(resid * resid) / length_x)
        update = precondition(
            resid, mode_eig, mean_cond, shift_re, shift_im, sine_y, sine_z, eig_y, eig_z
        )
        solution = solution + relax * update
    slabs = lax.all_to_all(solution, "gz", split_axis=1, concat_axis=2, tiled=True)
    result = transform(slabs, cos_t, sin_t, True)
    sums = jnp.sum(lax.all_gather(jnp.stack(partials)[None, :], "gz", axis=0, tiled=True), axis=0)
    return (result, jnp.sqrt(sums / cells))


RADIX = 4


def halves(table):
    high = table.astype(jnp.bfloat16)
    low = (table - high.astype(np.float32)).astype(jnp.bfloat16)
    return (jnp.asarray(high), jnp.asarray(low))


def radix_tables(length_x):
    count = length_x // RADIX
    pos = np.arange(count)
    forward = []
    for residue in range(RADIX):
        modes = RADIX * pos + residue
        angle = 2.0 * np.pi / length_x * (modes[:, None] * pos[None, :] % length_x)
        cos_t, sin_t = np.cos(angle), np.sin(angle)
        forward.append(np.block([[cos_t, sin_t], [-sin_t, cos_t]]))
    forward = np.stack(forward)
    backward = np.swapaxes(forward, 1, 2) / length_x
    return (forward.astype(np.float32), backward.astype(np.float32))


def sine_host(length):
    indices = np.arange(length) + 1
    product = indices[:, None] * indices[None, :] % (2 * (length + 1))
    return (np.sqrt(2.0 / (length + 1)) * np.sin(np.pi / (length + 1) * product)).astype(np.float32)


def split(values):
    high = values.astype(jnp.bfloat16)
    return (high, (values - high.astype(jnp.float32)).astype(jnp.bfloat16))


def dot3(left, right):
    mul = functools.partial(jnp.dot, preferred_element_type=jnp.float32)
    return mul(left[0], right[0]) + (mul(left[0], right[1]) + mul(left[1], right[0]))


def turn(re, im, quarter):
    quarter = quarter % 4
    return [(re, im), (-im, re), (-re, -im), (im, -re)][quarter]


def combine(parts, quarters):
    re, im = turn(*parts[0], quarters[0])
    for part, quarter in zip(parts[1:], quarters[1:]):
        more_re, more_im = turn(*part, quarter)
        re, im = re + more_re, im + more_im
    return (re, im)


def times(left, right):
    return (left[0] * right[0] - left[1] * right[1], left[0] * right[1] + left[1] * right[0])


def plus(left, right):
    return (left[0] + right[0], left[1] + right[1])


def kernel(
    groups,
    planes,
    chunks,
    source_hbm,
    conduct,
    mode_eig,
    base,
    shift,
    fwd_hi_hbm,
    fwd_lo_hbm,
    bwd_hi_hbm,
    bwd_lo_hbm,
    sine_hi_hbm,
    sine_lo_hbm,
    out,
    norms,
    source,
    fwd_hi,
    fwd_lo,
    bwd_hi,
    bwd_lo,
    sine_hi,
    sine_lo,
    spectra,
    forcing,
    cond_all,
    cond,
    work,
    alpha,
    lines,
    field,
    result,
    slabs,
    sums,
    squares,
    up_out,
    up_in,
    down_out,
    down_in,
    load_sem,
    in_send,
    in_recv,
    cond_send,
    cond_recv,
    out_send,
    out_recv,
    sum_send,
    sum_recv,
    up_send,
    up_recv,
    down_send,
    down_recv,
):
    me = lax.axis_index("gz")
    side = lax.rem(me, RADIX)
    team = me // RADIX
    teams = groups // RADIX
    length_x = source.shape[2]
    length_y = source.shape[3]
    length_z = groups * planes
    depth = RADIX * planes
    count = length_x // RADIX
    modes = count // chunks
    first_level = team * depth
    last_level = length_z - first_level - depth

    loads = [
        pltpu.make_async_copy(src, dst, load_sem.at[index])
        for index, (src, dst) in enumerate(
            [
                (source_hbm, source),
                (fwd_hi_hbm, fwd_hi),
                (fwd_lo_hbm, fwd_lo),
                (sine_hi_hbm, sine_hi),
                (sine_lo_hbm, sine_lo),
                (bwd_hi_hbm, bwd_hi),
                (bwd_lo_hbm, bwd_lo),
            ]
        )
    ]
    for load in loads:
        load.start()

    def remote(src, dst, send, recv, target):
        return pltpu.make_async_remote_copy(
            src_ref=src,
            dst_ref=dst,
            send_sem=send,
            recv_sem=recv,
            device_id={"gz": target},
            device_id_type=pl.DeviceIdType.MESH,
        )

    def peer(offset):
        return lax.rem(me + offset, groups)

    def mate(offset):
        return lax.rem(side + offset, RADIX)

    def rows(index):
        return pl.ds(index * planes, planes)

    def cond_copy(offset):
        return remote(
            conduct, cond_all.at[me], cond_send.at[offset], cond_recv.at[offset], peer(offset)
        )

    def sum_copy(offset):
        return remote(
            sums.at[me], sums.at[me], sum_send.at[offset], sum_recv.at[offset], peer(offset)
        )

    def in_copy(chunk, offset):
        target = mate(offset)
        return remote(
            spectra.at[target, chunk],
            forcing.at[chunk, rows(side)],
            in_send.at[chunk, offset],
            in_recv.at[chunk, offset],
            team * RADIX + target,
        )

    def out_copy(chunk, offset):
        target = mate(offset)
        return remote(
            result.at[chunk, rows(target)],
            slabs.at[side, chunk],
            out_send.at[chunk, offset],
            out_recv.at[chunk, offset],
            team * RADIX + target,
        )

    def up_copy(turn_id, chunk, source_team, target_team):
        return remote(
            up_out.at[turn_id, chunk],
            up_in.at[turn_id, chunk, source_team],
            up_send.at[turn_id, chunk, target_team],
            up_recv.at[turn_id, chunk, source_team],
            target_team * RADIX + side,
        )

    def down_copy(turn_id, chunk, source_team, target_team):
        return remote(
            down_out.at[turn_id, chunk],
            down_in.at[turn_id, chunk, source_team],
            down_send.at[turn_id, chunk, target_team],
            down_recv.at[turn_id, chunk, source_team],
            target_team * RADIX + side,
        )

    def loop(first, stop, act):
        def run(index, carry):
            act(index)
            return carry

        lax.fori_loop(first, stop, run, 0)

    def each_peer(act):
        def run(offset, carry):
            act(offset)
            return carry

        lax.fori_loop(1, groups, run, 0)

    def pair(ref, *index):
        return (ref[(*index, 0)], ref[(*index, 1)])

    def put(ref, values, *index):
        ref[(*index, 0)] = values[0]
        ref[(*index, 1)] = values[1]

    barrier = pltpu.get_barrier_semaphore()

    @each_peer
    def _(offset):
        pl.semaphore_signal(
            barrier, inc=1, device_id={"gz": peer(offset)}, device_id_type=pl.DeviceIdType.MESH
        )

    pl.semaphore_wait(barrier, groups - 1)

    @each_peer
    def _(offset):
        cond_copy(offset).start()

    cond_all[me] = conduct[...]
    for load in loads[:3]:
        load.wait()

    def forward(plane, carry):
        parts = [
            (
                source[0, plane, q * count : (q + 1) * count, :],
                source[1, plane, q * count : (q + 1) * count, :],
            )
            for q in range(RADIX)
        ]
        for residue in range(RADIX):
            mixed = combine(parts, [-residue * q for q in range(RADIX)])
            right = split(jnp.concatenate(mixed, axis=0))
            values = dot3((fwd_hi[residue], fwd_lo[residue]), right)
            for chunk in range(chunks):
                for part in range(2):
                    start = part * count + chunk * modes
                    spectra[residue, chunk, plane, part] = values[start : start + modes]
        return carry

    lax.fori_loop(0, planes, forward, 0)
    for chunk in range(chunks):
        for offset in (2, 3, 1):
            in_copy(chunk, offset).start()

    def keep(chunk, carry):
        forcing[chunk, rows(side)] = spectra[side, chunk]
        return carry

    lax.fori_loop(0, chunks, keep, 0)
    for load in loads[3:]:
        load.wait()

    @each_peer
    def _(offset):
        cond_copy(offset).wait()

    def spread(index, total):
        for plane in range(planes):
            row = jnp.broadcast_to(cond_all[index, plane : plane + 1, :], (8, length_y))
            cond[index * planes + plane + 1] = row
            total = total + row
        return total

    total = lax.fori_loop(0, groups, spread, jnp.zeros((8, length_y), jnp.float32))
    cond[0] = cond[1]
    cond[length_z + 1] = cond[length_z]
    mean_cond = jnp.sum(total) / (8 * length_y * length_z)
    shift_re = shift[0]
    shift_im = shift[1]
    scale = relax / mean_cond
    offset_re = shift_re / mean_cond
    diag_im = shift_im / mean_cond
    none = jnp.zeros((modes, length_y), jnp.float32)
    one = jnp.ones((modes, length_y), jnp.float32)

    def factors(chunk):
        diag_re = base[chunk] + offset_re

        def factor(level, carry):
            gap_re = diag_re - carry[0]
            gap_im = diag_im - carry[1]
            inverse = 1.0 / (gap_re * gap_re + gap_im * gap_im)
            now = (gap_re * inverse, -gap_im * inverse)
            put(alpha, now, chunk, level)
            return now

        def segment(index, carry):
            def inner(level, state):
                now = factor(index * depth + level + 1, state[:2])
                return (*now, *times(now, state[2:]))

            state = lax.fori_loop(0, depth, inner, (*carry, one, none))
            put(lines, state[2:], chunk, index)
            return state[:2]

        put(alpha, (none, none), chunk, 0)
        lax.fori_loop(0, teams, segment, (none, none))

    sine = (sine_hi[...], sine_lo[...])

    def sine_rows(values):
        flat = values.reshape(values.shape[0] * 2 * modes, length_y)
        return dot3(split(flat), sine).reshape(values.shape)

    def launch(turn_id, chunk):
        def rise(index, carry):
            factor = pair(alpha, chunk, first_level + index + 1)
            return times(factor, plus(pair(work, chunk, index), carry))

        put(up_out, lax.fori_loop(0, depth, rise, (none, none)), turn_id, chunk)
        loop(team + 1, teams, lambda target: up_copy(turn_id, chunk, team, target).start())

        def fall(index, carry):
            factor = pair(alpha, chunk, last_level + index + 1)
            return times(factor, plus(pair(work, chunk, depth - 1 - index), carry))

        put(down_out, lax.fori_loop(0, depth, fall, (none, none)), turn_id, chunk)
        loop(0, team, lambda target: down_copy(turn_id, chunk, team, target).start())

    def solve(turn_id, chunk):
        def gather_up(index, carry):
            up_copy(turn_id, chunk, index, team).wait_recv()
            return plus(pair(up_in, turn_id, chunk, index), times(pair(lines, chunk, index), carry))

        def gather_down(index, carry):
            origin = teams - 1 - index
            down_copy(turn_id, chunk, origin, team).wait_recv()
            more = times(pair(lines, chunk, index), carry)
            return plus(pair(down_in, turn_id, chunk, origin), more)

        below = lax.fori_loop(0, team, gather_up, (none, none))
        above = lax.fori_loop(0, teams - 1 - team, gather_down, (none, none))

        def ahead(index, carry):
            factor = pair(alpha, chunk, first_level + index + 1)
            now = times(factor, plus(pair(work, chunk, index), carry))
            put(work, now, chunk, index)
            return now

        reached = lax.fori_loop(0, depth, ahead, below)
        factor = pair(alpha, chunk, first_level + depth)
        edge = pair(alpha, chunk, last_level)
        echo = times(factor, edge)
        gap_re = 1.0 - echo[0]
        inverse = 1.0 / (gap_re * gap_re + echo[1] * echo[1])
        top = plus(reached, times(factor, above))
        top = times(top, (gap_re * inverse, echo[1] * inverse))
        outer = plus(above, times(edge, top))
        put(work, outer, chunk, depth + 1)

        def behind(step, carry):
            index = depth - 1 - step
            factor = pair(alpha, chunk, first_level + index + 1)
            now = plus(pair(work, chunk, index), times(factor, carry))
            put(work, now, chunk, index)
            return now

        bottom = lax.fori_loop(0, depth, behind, outer)
        put(work, plus(below, times(pair(alpha, chunk, first_level), bottom)), chunk, depth)

    lane = lax.broadcasted_iota(jnp.int32, (modes, length_y), 1)
    row_lane = lax.broadcasted_iota(jnp.int32, (8, length_y), 1)
    last = length_y - 1

    def residual(chunk):
        def run(index, carry):
            level = first_level + index
            here = cond[level + 1]
            right = jnp.where(row_lane == last, here, pltpu.roll(here, last, 1))
            left = jnp.where(row_lane == 0, here, pltpu.roll(here, 1, 1))
            face_yp = (0.5 * (here + right))[0:1]
            face_ym = (0.5 * (here + left))[0:1]
            face_zp = (0.5 * (here + cond[level + 2]))[0:1]
            face_zm = (0.5 * (here + cond[level]))[0:1]
            center = here[0:1] * mode_eig[chunk] + (face_yp + face_ym + face_zp + face_zm)
            center = center + shift_re
            values = pair(field, chunk, index + 1)
            turned = (-shift_im * values[1], shift_im * values[0])
            above = pair(field, chunk, index + 2)
            below = pair(field, chunk, index)
            for part in range(2):
                value = values[part]
                right = jnp.where(lane == last, 0.0, pltpu.roll(value, last, 1))
                left = jnp.where(lane == 0, 0.0, pltpu.roll(value, 1, 1))
                applied = center * value + turned[part]
                applied = applied - face_yp * right - face_ym * left
                applied = applied - face_zp * above[part] - face_zm * below[part]
                given = forcing[chunk, index, part]
                rest = given - applied
                work[chunk, index, part] = rest
                squares[0] = squares[0] + given * given
                squares[1] = squares[1] + rest * rest
            return carry

        lax.fori_loop(0, depth, run, 0)

    squares[0] = none
    squares[1] = none

    def step(index, carry):
        @pl.when(index < chunks)
        def _():
            chunk = index
            factors(chunk)
            for offset in range(1, RADIX):
                in_copy(chunk, offset).wait()
            work[chunk, pl.ds(0, depth)] = sine_rows(forcing[chunk])
            launch(0, chunk)

        @pl.when((index >= 1) & (index < chunks + 1))
        def _():
            chunk = index - 1
            solve(0, chunk)
            values = sine_rows(work[chunk]) * scale
            field[chunk, pl.ds(1, depth)] = values[:depth]
            field[chunk, 0] = values[depth]
            field[chunk, depth + 1] = values[depth + 1]
            residual(chunk)
            work[chunk, pl.ds(0, depth)] = sine_rows(work[chunk, pl.ds(0, depth)])
            launch(1, chunk)

        @pl.when(index >= 2)
        def _():
            chunk = index - 2
            solve(1, chunk)
            values = sine_rows(work[chunk, pl.ds(0, depth)]) * scale
            result[chunk] = field[chunk, pl.ds(1, depth)] + values
            for offset in (2, 3, 1):
                out_copy(chunk, offset).start()
            slabs[side, chunk] = result[chunk, rows(side)]

        return carry

    lax.fori_loop(0, chunks + 2, step, 0)
    row = lax.broadcasted_iota(jnp.int32, (8, 128), 0)
    sums[me] = jnp.where(row == 0, jnp.sum(squares[0]), jnp.sum(squares[1])) / length_x

    @each_peer
    def _(offset):
        sum_copy(offset).start()

    def settle_sends(index, carry):
        for turn_id in range(2):
            loop(team + 1, teams, lambda target: up_copy(turn_id, index, team, target).wait_send())
            loop(0, team, lambda target: down_copy(turn_id, index, team, target).wait_send())
        return carry

    lax.fori_loop(0, chunks, settle_sends, 0)

    @each_peer
    def _(offset):
        sum_copy(offset).wait()

    norms[...] = jnp.sum(sums[...], axis=0)

    def settle_out(index, carry):
        for offset in range(1, RADIX):
            out_copy(index, offset).wait()
        return carry

    lax.fori_loop(0, chunks, settle_out, 0)

    def inverse(plane, carry):
        parts = []
        for residue in range(RADIX):
            blocks = [
                slabs[residue, chunk, plane, part] for part in range(2) for chunk in range(chunks)
            ]
            right = split(jnp.concatenate(blocks, axis=0))
            values = dot3((bwd_hi[residue], bwd_lo[residue]), right)
            parts.append((values[:count], values[count:]))
        for q in range(RADIX):
            re, im = combine(parts, [residue * q for residue in range(RADIX)])
            out[0, plane, q * count : (q + 1) * count, :] = re
            out[1, plane, q * count : (q + 1) * count, :] = im
        return carry

    lax.fori_loop(0, planes, inverse, 0)


CHUNKS = 4


def body(source, layer_ids, conduct_table, shift):
    planes = source.shape[1]
    length_x = source.shape[2]
    length_y = source.shape[3]
    groups = lax.axis_size("gz")
    length_z = planes * groups
    count = length_x // RADIX
    modes = count // CHUNKS
    if groups % RADIX or groups < 2 * RADIX or modes % 8 or planes > 8 or length_z > 64:
        return body_plain(source, layer_ids, conduct_table, shift)
    me = lax.axis_index("gz")
    depth = planes * RADIX
    layers = conduct_table.shape[0]
    onehot = layer_ids[:, :, None] == lax.iota(jnp.int32, layers)[None, None, :]
    conduct = jnp.sum(jnp.where(onehot, conduct_table[None, None, :], 0.0), axis=-1)
    conduct = jnp.pad(conduct, ((0, 8 - planes), (0, 0)))
    mode_ids = RADIX * lax.iota(jnp.int32, count) + me % RADIX
    mode_eig = 2.0 - 2.0 * jnp.cos(2.0 * jnp.pi / length_x * mode_ids.astype(jnp.float32))
    mode_eig = jnp.broadcast_to(mode_eig[:, None], (count, length_y))
    base = mode_eig + (sine_eigen(length_y) + 2.0)[None, :]
    mode_eig = mode_eig.reshape(CHUNKS, modes, length_y)
    base = base.reshape(CHUNKS, modes, length_y)
    forward, backward = radix_tables(length_x)
    tables = [*halves(forward), *halves(backward), *halves(sine_host(length_y))]
    tile = (2, modes, length_y)
    vmem = pl.BlockSpec(memory_space=pltpu.VMEM)
    hbm = pl.BlockSpec(memory_space=pl.ANY)
    f32 = jnp.float32
    result, norms = pl.pallas_call(
        functools.partial(kernel, groups, planes, CHUNKS),
        out_shape=(
            jax.ShapeDtypeStruct(source.shape, f32),
            jax.ShapeDtypeStruct((8, 128), f32),
        ),
        in_specs=[hbm] + [vmem] * 3 + [pl.BlockSpec(memory_space=pltpu.SMEM)] + [hbm] * 6,
        out_specs=(vmem, vmem),
        scratch_shapes=[pltpu.VMEM(source.shape, f32)]
        + [pltpu.VMEM(table.shape, jnp.bfloat16) for table in tables]
        + [
            pltpu.VMEM((RADIX, CHUNKS, planes, *tile), f32),
            pltpu.VMEM((CHUNKS, depth, *tile), f32),
            pltpu.VMEM((groups, 8, length_y), f32),
            pltpu.VMEM((length_z + 2, 8, length_y), f32),
            pltpu.VMEM((CHUNKS, depth + 2, *tile), f32),
            pltpu.VMEM((CHUNKS, length_z + 1, *tile), f32),
            pltpu.VMEM((CHUNKS, groups // RADIX, *tile), f32),
            pltpu.VMEM((CHUNKS, depth + 2, *tile), f32),
            pltpu.VMEM((CHUNKS, depth, *tile), f32),
            pltpu.VMEM((RADIX, CHUNKS, planes, *tile), f32),
            pltpu.VMEM((groups, 8, 128), f32),
            pltpu.VMEM(tile, f32),
        ]
        + [
            pltpu.VMEM((ITERS, CHUNKS, *tile), f32),
            pltpu.VMEM((ITERS, CHUNKS, groups // RADIX, *tile), f32),
        ]
        * 2
        + [pltpu.SemaphoreType.DMA((7,))]
        + [pltpu.SemaphoreType.DMA((CHUNKS, RADIX))] * 2
        + [pltpu.SemaphoreType.DMA((groups,))] * 2
        + [pltpu.SemaphoreType.DMA((CHUNKS, RADIX))] * 2
        + [pltpu.SemaphoreType.DMA((groups,))] * 2
        + [pltpu.SemaphoreType.DMA((ITERS, CHUNKS, groups // RADIX))] * 4,
        compiler_params=pltpu.CompilerParams(
            collective_id=0, has_side_effects=True, vmem_limit_bytes=58 << 20
        ),
    )(source, conduct, mode_eig, base, shift, *tables)
    cells = length_x * length_y * length_z
    return (result, jnp.sqrt(norms[:ITERS, 0] / cells))


def solution(mesh):
    placed = (P(None, ("node", "gz"), None, None), P(("node", "gz"), None), P(), P("node"))
    return jax.shard_map(
        body,
        mesh=mesh,
        in_specs=placed,
        out_specs=(P(None, ("node", "gz"), None, None), P("node")),
        check_vma=False,
    )
```

profile of v0, /device:TPU:1, one launch (start us, length us, event | category | flops | bytes accessed | tf_op | source)
XLA Modules:
  0.0 85.0 jit_solution(9699420135006466780)
XLA Ops:
  0.7 0.8 select_reduce_fusion
  1.5 0.6 pad.4.conduct
  2.1 0.7 broadcast_add_fusion.base
  2.9 0.7 broadcast_in_dim.24.mode_eig
  3.6 77.0 %shard_map.113 = (f32[2,2,512,256]{3,2,1,0:T(8,128)}, f32[8,128]{1,0:T(8,128)}) custom-call(f32[2,2,512,256]{3,2,1,0:T(8,128)} %source_hbm.1, f32[8,256]{1,0:T(8,128)} %pad.4.conduct, f32[4,32,256]{2,1,0:T(8,128)} %broadcast_in_dim.24.mode_eig, f32[4,32,256]{2,1,0:T(8,128)} %broadcast_add_fusion.base, f32[2]{0:T(128)} %shift.1, ...), custom_call_target="tpu_custom_call" | custom-call | tf_op jit(solution)/shard_map/pallas_call | solution.py:700
  80.6 1.3 %sqrt_reduce_fusion = f32[2]{0:T(128)} fusion(f32[8,128]{1,0:T(8,128)} %get-tuple-element.5), kind=kLoop, calls=%fused_computation.4 | loop fusion | flops 2 | bytes 16 | tf_op jit(solution)/shard_map/sqrt | solution.py:740
  81.9 3.0 %copy.13 = f32[2,2,512,256]{3,2,1,0:T(8,128)} copy(f32[2,2,512,256]{3,2,1,0:T(8,128)} %get-tuple-element.8) | data formatting | bytes 4194304
  (2 shorter events, 0.1 us)
where the time goes:
time: 85.6 us; the launch traced here: 85 us
  Pallas kernels  77 us (90%)
  local copies, waits for them, and re-layouts  4.38 us (5%)
  other arithmetic  2.94 us (3%)
    pallas_call x1, Pallas kernels, body(): pl.pallas_call(functools.partial(kernel, groups, planes, CHUNKS), out_sha...  77 us
    unnamed x1, local copies, waits for them, and re-layouts  3.04 us

commit v1 on v0

--- a/solution.py
+++ b/solution.py
@@ -217,46 +217,62 @@
     return (left[0] + right[0], left[1] + right[1])
 
 
+def pair(ref, *index):
+    return (ref[(*index, 0)], ref[(*index, 1)])
+
+
+def put(ref, values, *index):
+    ref[(*index, 0)] = values[0]
+    ref[(*index, 1)] = values[1]
+
+
+def choose(test, left, right):
+    return (jnp.where(test, left[0], right[0]), jnp.where(test, left[1], right[1]))
+
+
 def kernel(
     groups,
     planes,
     chunks,
+    layers,
     source_hbm,
-    conduct,
-    mode_eig,
-    base,
+    ids_hbm,
+    table,
     shift,
+    mode_hbm,
+    eig_hbm,
     fwd_hi_hbm,
     fwd_lo_hbm,
-    bwd_hi_hbm,
-    bwd_lo_hbm,
     sine_hi_hbm,
     sine_lo_hbm,
-    out,
-    norms,
+    slabs,
+    sums,
     source,
+    ids,
+    mode_eig,
+    eig_y,
     fwd_hi,
     fwd_lo,
-    bwd_hi,
-    bwd_lo,
     sine_hi,
     sine_lo,
     spectra,
     forcing,
+    cond_own,
     cond_all,
     cond,
+    faces,
     work,
     alpha,
     lines,
     field,
     result,
-    slabs,
-    sums,
+    sum_own,
     squares,
-    up_out,
-    up_in,
-    down_out,
-    down_in,
+    pair_out,
+    pair_in,
+    rest_out,
+    comb_out,
+    comb_in,
     load_sem,
     in_send,
     in_recv,
@@ -266,10 +282,11 @@
     out_recv,
     sum_send,
     sum_recv,
-    up_send,
-    up_recv,
-    down_send,
-    down_recv,
+    own_sem,
+    pair_send,
+    pair_recv,
+    comb_send,
+    comb_recv,
 ):
     me = lax.axis_index("gz")
     side = lax.rem(me, RADIX)
@@ -291,14 +308,15 @@
                 (source_hbm, source),
                 (fwd_hi_hbm, fwd_hi),
                 (fwd_lo_hbm, fwd_lo),
+                (ids_hbm, ids),
+                (mode_hbm.at[side], mode_eig),
+                (eig_hbm, eig_y),
                 (sine_hi_hbm, sine_hi),
                 (sine_lo_hbm, sine_lo),
-                (bwd_hi_hbm, bwd_hi),
-                (bwd_lo_hbm, bwd_lo),
             ]
         )
     ]
-    for load in loads:
+    for load in [loads[3], *loads[:3], *loads[4:]]:
         load.start()
 
     def remote(src, dst, send, recv, target):
@@ -322,12 +340,12 @@
 
     def cond_copy(offset):
         return remote(
-            conduct, cond_all.at[me], cond_send.at[offset], cond_recv.at[offset], peer(offset)
+            cond_own, cond_all.at[me], cond_send.at[offset], cond_recv.at[offset], peer(offset)
         )
 
     def sum_copy(offset):
         return remote(
-            sums.at[me], sums.at[me], sum_send.at[offset], sum_recv.at[offset], peer(offset)
+            sum_own, sums.at[me], sum_send.at[offset], sum_recv.at[offset], peer(offset)
         )
 
     def in_copy(chunk, offset):
@@ -350,30 +368,34 @@
             team * RADIX + target,
         )
 
-    def up_copy(turn_id, chunk, source_team, target_team):
+    def own_copy(chunk):
+        return pltpu.make_async_copy(
+            result.at[chunk, rows(side)], slabs.at[side, chunk], own_sem.at[chunk]
+        )
+
+    even = lax.rem(team, 2) == 0
+    inner = (team == 1) | (team == 2)
+    lower = team < 2
+    partner = team + 1 - 2 * lax.rem(team, 2)
+
+    def pair_copy(turn_id, chunk):
         return remote(
-            up_out.at[turn_id, chunk],
-            up_in.at[turn_id, chunk, source_team],
-            up_send.at[turn_id, chunk, target_team],
-            up_recv.at[turn_id, chunk, source_team],
-            target_team * RADIX + side,
-        )
-
-    def down_copy(turn_id, chunk, source_team, target_team):
+            pair_out.at[turn_id, chunk],
+            pair_in.at[turn_id, chunk],
+            pair_send.at[turn_id, chunk],
+            pair_recv.at[turn_id, chunk],
+            partner * RADIX + side,
+        )
+
+    def comb_copy(turn_id, chunk, which):
+        target = [teams - 1 - team, (teams - 1) * (2 - team)][which]
         return remote(
-            down_out.at[turn_id, chunk],
-            down_in.at[turn_id, chunk, source_team],
-            down_send.at[turn_id, chunk, target_team],
-            down_recv.at[turn_id, chunk, source_team],
-            target_team * RADIX + side,
-        )
-
-    def loop(first, stop, act):
-        def run(index, carry):
-            act(index)
-            return carry
-
-        lax.fori_loop(first, stop, run, 0)
+            comb_out.at[turn_id, chunk],
+            comb_in.at[turn_id, chunk],
+            comb_send.at[turn_id, chunk, which],
+            comb_recv.at[turn_id, chunk],
+            target * RADIX + side,
+        )
 
     def each_peer(act):
         def run(offset, carry):
@@ -382,13 +404,6 @@
 
         lax.fori_loop(1, groups, run, 0)
 
-    def pair(ref, *index):
-        return (ref[(*index, 0)], ref[(*index, 1)])
-
-    def put(ref, values, *index):
-        ref[(*index, 0)] = values[0]
-        ref[(*index, 1)] = values[1]
-
     barrier = pltpu.get_barrier_semaphore()
 
     @each_peer
@@ -397,13 +412,12 @@
             barrier, inc=1, device_id={"gz": peer(offset)}, device_id_type=pl.DeviceIdType.MESH
         )
 
-    pl.semaphore_wait(barrier, groups - 1)
-
-    @each_peer
-    def _(offset):
-        cond_copy(offset).start()
-
-    cond_all[me] = conduct[...]
+    loads[3].wait()
+    found = jnp.zeros((planes, length_y), jnp.float32)
+    for layer in range(layers):
+        found = found + jnp.where(ids[...] == layer, table[layer], 0.0)
+    cond_own[...] = found
+    cond_all[me] = found
     for load in loads[:3]:
         load.wait()
 
@@ -426,16 +440,25 @@
         return carry
 
     lax.fori_loop(0, planes, forward, 0)
-    for chunk in range(chunks):
+    pl.semaphore_wait(barrier, groups - 1)
+
+    @each_peer
+    def _(offset):
+        cond_copy(offset).start()
+
+    def send_in(chunk, carry):
         for offset in (2, 3, 1):
             in_copy(chunk, offset).start()
+        return carry
+
+    lax.fori_loop(0, chunks, send_in, 0)
 
     def keep(chunk, carry):
         forcing[chunk, rows(side)] = spectra[side, chunk]
         return carry
 
     lax.fori_loop(0, chunks, keep, 0)
-    for load in loads[3:]:
+    for load in loads[4:]:
         load.wait()
 
     @each_peer
@@ -460,9 +483,33 @@
     diag_im = shift_im / mean_cond
     none = jnp.zeros((modes, length_y), jnp.float32)
     one = jnp.ones((modes, length_y), jnp.float32)
+    row_lane = lax.broadcasted_iota(jnp.int32, (8, length_y), 1)
+    last = length_y - 1
+
+    def make_faces(index, carry):
+        level = first_level + index
+        here = cond[level + 1]
+        right = jnp.where(row_lane == last, here, pltpu.roll(here, last, 1))
+        left = jnp.where(row_lane == 0, here, pltpu.roll(here, 1, 1))
+        face_yp = 0.5 * (here + right)
+        face_ym = 0.5 * (here + left)
+        face_zp = 0.5 * (here + cond[level + 2])
+        face_zm = 0.5 * (here + cond[level])
+        faces[index, 0] = here
+        faces[index, 1] = face_yp + face_ym + face_zp + face_zm + shift_re
+        faces[index, 2] = jnp.where(row_lane == last, 0.0, face_yp)
+        faces[index, 3] = jnp.where(row_lane == 0, 0.0, face_ym)
+        faces[index, 4] = face_zp
+        faces[index, 5] = face_zm
+        return carry
+
+    lax.fori_loop(0, depth, make_faces, 0)
+
+    def eigen(chunk):
+        return jnp.concatenate([mode_eig[chunk]] * (length_y // 128), axis=1)
 
     def factors(chunk):
-        diag_re = base[chunk] + offset_re
+        diag_re = eigen(chunk) + (eig_y[0:1, :] + offset_re)
 
         def factor(level, carry):
             gap_re = diag_re - carry[0]
@@ -473,11 +520,11 @@
             return now
 
         def segment(index, carry):
-            def inner(level, state):
+            def inner_level(level, state):
                 now = factor(index * depth + level + 1, state[:2])
                 return (*now, *times(now, state[2:]))
 
-            state = lax.fori_loop(0, depth, inner, (*carry, one, none))
+            state = lax.fori_loop(0, depth, inner_level, (*carry, one, none))
             put(lines, state[2:], chunk, index)
             return state[:2]
 
@@ -492,32 +539,40 @@
 
     def launch(turn_id, chunk):
         def rise(index, carry):
-            factor = pair(alpha, chunk, first_level + index + 1)
-            return times(factor, plus(pair(work, chunk, index), carry))
-
-        put(up_out, lax.fori_loop(0, depth, rise, (none, none)), turn_id, chunk)
-        loop(team + 1, teams, lambda target: up_copy(turn_id, chunk, team, target).start())
-
-        def fall(index, carry):
-            factor = pair(alpha, chunk, last_level + index + 1)
-            return times(factor, plus(pair(work, chunk, depth - 1 - index), carry))
-
-        put(down_out, lax.fori_loop(0, depth, fall, (none, none)), turn_id, chunk)
-        loop(0, team, lambda target: down_copy(turn_id, chunk, team, target).start())
+            up = times(
+                pair(alpha, chunk, first_level + index + 1),
+                plus(pair(work, chunk, index), carry[:2]),
+            )
+            down = times(
+                pair(alpha, chunk, last_level + index + 1),
+                plus(pair(work, chunk, depth - 1 - index), carry[2:]),
+            )
+            return (*up, *down)
+
+        ends = lax.fori_loop(0, depth, rise, (none, none, none, none))
+        put(pair_out, choose(even, ends[:2], ends[2:]), turn_id, chunk)
+        pair_copy(turn_id, chunk).start()
+        put(rest_out, choose(even, ends[2:], ends[:2]), turn_id, chunk)
+
+    def relay(turn_id, chunk):
+        pair_copy(turn_id, chunk).wait_recv()
+
+        @pl.when(inner)
+        def _():
+            more = times(pair(lines, chunk, 1), pair(pair_in, turn_id, chunk))
+            put(comb_out, plus(pair(rest_out, turn_id, chunk), more), turn_id, chunk)
+            comb_copy(turn_id, chunk, 1).start()
+            comb_copy(turn_id, chunk, 0).start()
 
     def solve(turn_id, chunk):
-        def gather_up(index, carry):
-            up_copy(turn_id, chunk, index, team).wait_recv()
-            return plus(pair(up_in, turn_id, chunk, index), times(pair(lines, chunk, index), carry))
-
-        def gather_down(index, carry):
-            origin = teams - 1 - index
-            down_copy(turn_id, chunk, origin, team).wait_recv()
-            more = times(pair(lines, chunk, index), carry)
-            return plus(pair(down_in, turn_id, chunk, origin), more)
-
-        below = lax.fori_loop(0, team, gather_up, (none, none))
-        above = lax.fori_loop(0, teams - 1 - team, gather_down, (none, none))
+        comb_copy(turn_id, chunk, 0).wait_recv()
+        near = pair(pair_in, turn_id, chunk)
+        wide = pair(comb_in, turn_id, chunk)
+        joined = plus(near, times(pair(lines, chunk, teams - 2), wide))
+        far = choose(inner, wide, joined)
+        near = choose(inner, near, (none, none))
+        below = choose(lower, near, far)
+        above = choose(lower, far, near)
 
         def ahead(index, carry):
             factor = pair(alpha, chunk, first_level + index + 1)
@@ -546,58 +601,69 @@
         bottom = lax.fori_loop(0, depth, behind, outer)
         put(work, plus(below, times(pair(alpha, chunk, first_level), bottom)), chunk, depth)
 
-    lane = lax.broadcasted_iota(jnp.int32, (modes, length_y), 1)
-    row_lane = lax.broadcasted_iota(jnp.int32, (8, length_y), 1)
-    last = length_y - 1
+    def blocks(values):
+        return values.reshape(modes // 8, 8, length_y)
 
     def residual(chunk):
+        eig = blocks(eigen(chunk))
+
         def run(index, carry):
-            level = first_level + index
-            here = cond[level + 1]
-            right = jnp.where(row_lane == last, here, pltpu.roll(here, last, 1))
-            left = jnp.where(row_lane == 0, here, pltpu.roll(here, 1, 1))
-            face_yp = (0.5 * (here + right))[0:1]
-            face_ym = (0.5 * (here + left))[0:1]
-            face_zp = (0.5 * (here + cond[level + 2]))[0:1]
-            face_zm = (0.5 * (here + cond[level]))[0:1]
-            center = here[0:1] * mode_eig[chunk] + (face_yp + face_ym + face_zp + face_zm)
-            center = center + shift_re
+            given_sum, rest_sum = carry
+            center = faces[index, 0] * eig + faces[index, 1]
             values = pair(field, chunk, index + 1)
             turned = (-shift_im * values[1], shift_im * values[0])
             above = pair(field, chunk, index + 2)
             below = pair(field, chunk, index)
             for part in range(2):
                 value = values[part]
-                right = jnp.where(lane == last, 0.0, pltpu.roll(value, last, 1))
-                left = jnp.where(lane == 0, 0.0, pltpu.roll(value, 1, 1))
-                applied = center * value + turned[part]
-                applied = applied - face_yp * right - face_ym * left
-                applied = applied - face_zp * above[part] - face_zm * below[part]
+                applied = center * blocks(value) + blocks(turned[part])
+                applied = applied - faces[index, 2] * blocks(pltpu.roll(value, last, 1))
+                applied = applied - faces[index, 3] * blocks(pltpu.roll(value, 1, 1))
+                applied = applied - faces[index, 4] * blocks(above[part])
+                applied = applied - faces[index, 5] * blocks(below[part])
                 given = forcing[chunk, index, part]
-                rest = given - applied
+                rest = given - applied.reshape(modes, length_y)
                 work[chunk, index, part] = rest
-                squares[0] = squares[0] + given * given
-                squares[1] = squares[1] + rest * rest
-            return carry
-
-        lax.fori_loop(0, depth, run, 0)
+                given_sum = given_sum + given * given
+                rest_sum = rest_sum + rest * rest
+            return (given_sum, rest_sum)
+
+        given_sum, rest_sum = lax.fori_loop(0, depth, run, (none, none))
+        squares[0] = squares[0] + given_sum
+        squares[1] = squares[1] + rest_sum
 
     squares[0] = none
     squares[1] = none
+    factors(0)
 
     def step(index, carry):
         @pl.when(index < chunks)
         def _():
             chunk = index
-            factors(chunk)
             for offset in range(1, RADIX):
                 in_copy(chunk, offset).wait()
             work[chunk, pl.ds(0, depth)] = sine_rows(forcing[chunk])
             launch(0, chunk)
 
-        @pl.when((index >= 1) & (index < chunks + 1))
-        def _():
-            chunk = index - 1
+        def at(lag, act):
+            @pl.when((index >= lag) & (index < chunks + lag))
+            def _():
+                act(index - lag)
+
+        at(LAGS[0], functools.partial(relay, 0))
+        at(LAGS[2], functools.partial(relay, 1))
+
+        def finish(chunk):
+            solve(1, chunk)
+            values = sine_rows(work[chunk, pl.ds(0, depth)]) * scale
+            result[chunk] = field[chunk, pl.ds(1, depth)] + values
+            for offset in (2, 3, 1):
+                out_copy(chunk, offset).start()
+            own_copy(chunk).start()
+
+        at(LAGS[3], finish)
+
+        def middle(chunk):
             solve(0, chunk)
             values = sine_rows(work[chunk]) * scale
             field[chunk, pl.ds(1, depth)] = values[:depth]
@@ -607,50 +673,91 @@
             work[chunk, pl.ds(0, depth)] = sine_rows(work[chunk, pl.ds(0, depth)])
             launch(1, chunk)
 
-        @pl.when(index >= 2)
+        at(LAGS[1], middle)
+
+        @pl.when(index + 1 < chunks)
         def _():
-            chunk = index - 2
-            solve(1, chunk)
-            values = sine_rows(work[chunk, pl.ds(0, depth)]) * scale
-            result[chunk] = field[chunk, pl.ds(1, depth)] + values
-            for offset in (2, 3, 1):
-                out_copy(chunk, offset).start()
-            slabs[side, chunk] = result[chunk, rows(side)]
+            factors(index + 1)
+
+        @pl.when(index == chunks - 1 + LAGS[1])
+        def _():
+            row = lax.broadcasted_iota(jnp.int32, (ITERS, 128), 0)
+            both = jnp.where(row == 0, jnp.sum(squares[0]), jnp.sum(squares[1]))
+            sum_own[...] = both / length_x
+
+            @each_peer
+            def _(offset):
+                sum_copy(offset).start()
+
+            pltpu.make_async_copy(sum_own, sums.at[me], own_sem.at[chunks]).start()
 
         return carry
 
-    lax.fori_loop(0, chunks + 2, step, 0)
-    row = lax.broadcasted_iota(jnp.int32, (8, 128), 0)
-    sums[me] = jnp.where(row == 0, jnp.sum(squares[0]), jnp.sum(squares[1])) / length_x
-
-    @each_peer
-    def _(offset):
-        sum_copy(offset).start()
-
-    def settle_sends(index, carry):
+    lax.fori_loop(0, chunks + LAGS[3], step, 0)
+
+    def settle(chunk, carry):
         for turn_id in range(2):
-            loop(team + 1, teams, lambda target: up_copy(turn_id, index, team, target).wait_send())
-            loop(0, team, lambda target: down_copy(turn_id, index, team, target).wait_send())
+            pair_copy(turn_id, chunk).wait_send()
+
+            @pl.when(inner)
+            def _():
+                comb_copy(turn_id, chunk, 0).wait_send()
+                comb_copy(turn_id, chunk, 1).wait_send()
+
+        own_copy(chunk).wait()
+        for offset in range(1, RADIX):
+            out_copy(chunk, offset).wait()
         return carry
 
-    lax.fori_loop(0, chunks, settle_sends, 0)
+    pltpu.make_async_copy(sum_own, sums.at[me], own_sem.at[chunks]).wait()
 
     @each_peer
     def _(offset):
         sum_copy(offset).wait()
 
-    norms[...] = jnp.sum(sums[...], axis=0)
-
-    def settle_out(index, carry):
-        for offset in range(1, RADIX):
-            out_copy(index, offset).wait()
-        return carry
-
-    lax.fori_loop(0, chunks, settle_out, 0)
-
-    def inverse(plane, carry):
+    lax.fori_loop(0, chunks, settle, 0)
+
+
+def ending(
+    cells, slabs_hbm, bwd_hi_hbm, bwd_lo_hbm, sums, out, norms, slabs, bwd_hi, bwd_lo, stage, sem, out_sem
+):
+    chunks, planes, _, modes, length_y = slabs.shape[1:]
+    count = chunks * modes
+
+    def load(residue, plane):
+        return pltpu.make_async_copy(
+            slabs_hbm.at[residue, :, plane], slabs.at[residue, :, plane], sem.at[residue, plane]
+        )
+
+    tables = [
+        [
+            pltpu.make_async_copy(src.at[residue], dst.at[residue], sem.at[residue, planes + index])
+            for index, (src, dst) in enumerate([(bwd_hi_hbm, bwd_hi), (bwd_lo_hbm, bwd_lo)])
+        ]
+        for residue in range(RADIX)
+    ]
+    for residue in range(RADIX):
+        load(residue, 0).start()
+        for table in tables[residue]:
+            table.start()
+    for plane in range(1, planes):
+        for residue in range(RADIX):
+            load(residue, plane).start()
+
+    def store(plane, q):
+        return pltpu.make_async_copy(
+            stage.at[:, plane, pl.ds(q * count, count), :],
+            out.at[:, plane, pl.ds(q * count, count), :],
+            out_sem.at[plane, q],
+        )
+
+    for plane in range(planes):
         parts = []
         for residue in range(RADIX):
+            load(residue, plane).wait()
+            if plane == 0:
+                for table in tables[residue]:
+                    table.wait()
             blocks = [
                 slabs[residue, chunk, plane, part] for part in range(2) for chunk in range(chunks)
             ]
@@ -659,14 +766,19 @@
             parts.append((values[:count], values[count:]))
         for q in range(RADIX):
             re, im = combine(parts, [residue * q for residue in range(RADIX)])
-            out[0, plane, q * count : (q + 1) * count, :] = re
-            out[1, plane, q * count : (q + 1) * count, :] = im
-        return carry
-
-    lax.fori_loop(0, planes, inverse, 0)
-
-
-CHUNKS = 4
+            stage[0, plane, q * count : (q + 1) * count, :] = re
+            stage[1, plane, q * count : (q + 1) * count, :] = im
+            store(plane, q).start()
+    total = jnp.sqrt(jnp.sum(sums[...], axis=0) / cells)
+    for index in range(ITERS):
+        norms[index] = total[index, 0]
+    for plane in range(planes):
+        for q in range(RADIX):
+            store(plane, q).wait()
+
+
+CHUNKS = 8
+LAGS = (1, 3, 4, 6)
 
 
 def body(source, layer_ids, conduct_table, shift):
@@ -677,67 +789,87 @@
     length_z = planes * groups
     count = length_x // RADIX
     modes = count // CHUNKS
-    if groups % RADIX or groups < 2 * RADIX or modes % 8 or planes > 8 or length_z > 64:
+    if groups != 4 * RADIX or modes % 8 or planes > 8 or length_z > 64 or length_y % 128:
         return body_plain(source, layer_ids, conduct_table, shift)
-    me = lax.axis_index("gz")
     depth = planes * RADIX
     layers = conduct_table.shape[0]
-    onehot = layer_ids[:, :, None] == lax.iota(jnp.int32, layers)[None, None, :]
-    conduct = jnp.sum(jnp.where(onehot, conduct_table[None, None, :], 0.0), axis=-1)
-    conduct = jnp.pad(conduct, ((0, 8 - planes), (0, 0)))
-    mode_ids = RADIX * lax.iota(jnp.int32, count) + me % RADIX
-    mode_eig = 2.0 - 2.0 * jnp.cos(2.0 * jnp.pi / length_x * mode_ids.astype(jnp.float32))
-    mode_eig = jnp.broadcast_to(mode_eig[:, None], (count, length_y))
-    base = mode_eig + (sine_eigen(length_y) + 2.0)[None, :]
-    mode_eig = mode_eig.reshape(CHUNKS, modes, length_y)
-    base = base.reshape(CHUNKS, modes, length_y)
+    mode_ids = RADIX * np.arange(count)[None, :] + np.arange(RADIX)[:, None]
+    mode_eig = (2.0 - 2.0 * np.cos(2.0 * np.pi / length_x * mode_ids)).astype(np.float32)
+    mode_eig = np.broadcast_to(mode_eig[:, :, None], (RADIX, count, 128))
+    mode_eig = np.ascontiguousarray(mode_eig).reshape(RADIX, CHUNKS, modes, 128)
+    eig_y = 4.0 - 2.0 * np.cos(np.pi / (length_y + 1) * (np.arange(length_y) + 1.0))
+    eig_y = np.ascontiguousarray(np.broadcast_to(eig_y.astype(np.float32), (8, length_y)))
     forward, backward = radix_tables(length_x)
-    tables = [*halves(forward), *halves(backward), *halves(sine_host(length_y))]
+    tables = [*halves(forward), *halves(sine_host(length_y))]
     tile = (2, modes, length_y)
-    vmem = pl.BlockSpec(memory_space=pltpu.VMEM)
+    smem = pl.BlockSpec(memory_space=pltpu.SMEM)
     hbm = pl.BlockSpec(memory_space=pl.ANY)
     f32 = jnp.float32
-    result, norms = pl.pallas_call(
-        functools.partial(kernel, groups, planes, CHUNKS),
+    dma = pltpu.SemaphoreType.DMA
+    slabs, sums = pl.pallas_call(
+        functools.partial(kernel, groups, planes, CHUNKS, layers),
         out_shape=(
-            jax.ShapeDtypeStruct(source.shape, f32),
-            jax.ShapeDtypeStruct((8, 128), f32),
+            jax.ShapeDtypeStruct((RADIX, CHUNKS, planes, *tile), f32),
+            jax.ShapeDtypeStruct((groups, ITERS, 128), f32),
         ),
-        in_specs=[hbm] + [vmem] * 3 + [pl.BlockSpec(memory_space=pltpu.SMEM)] + [hbm] * 6,
-        out_specs=(vmem, vmem),
-        scratch_shapes=[pltpu.VMEM(source.shape, f32)]
+        in_specs=[hbm] * 2 + [smem] * 2 + [hbm] * 6,
+        out_specs=(hbm, hbm),
+        scratch_shapes=[
+            pltpu.VMEM(source.shape, f32),
+            pltpu.VMEM(layer_ids.shape, jnp.int32),
+            pltpu.VMEM((CHUNKS, modes, 128), f32),
+            pltpu.VMEM((8, length_y), f32),
+        ]
         + [pltpu.VMEM(table.shape, jnp.bfloat16) for table in tables]
         + [
             pltpu.VMEM((RADIX, CHUNKS, planes, *tile), f32),
             pltpu.VMEM((CHUNKS, depth, *tile), f32),
-            pltpu.VMEM((groups, 8, length_y), f32),
+            pltpu.VMEM((planes, length_y), f32),
+            pltpu.VMEM((groups, planes, length_y), f32),
             pltpu.VMEM((length_z + 2, 8, length_y), f32),
+            pltpu.VMEM((depth, 6, 8, length_y), f32),
             pltpu.VMEM((CHUNKS, depth + 2, *tile), f32),
             pltpu.VMEM((CHUNKS, length_z + 1, *tile), f32),
             pltpu.VMEM((CHUNKS, groups // RADIX, *tile), f32),
             pltpu.VMEM((CHUNKS, depth + 2, *tile), f32),
             pltpu.VMEM((CHUNKS, depth, *tile), f32),
-            pltpu.VMEM((RADIX, CHUNKS, planes, *tile), f32),
-            pltpu.VMEM((groups, 8, 128), f32),
+            pltpu.VMEM((ITERS, 128), f32),
             pltpu.VMEM(tile, f32),
         ]
-        + [
-            pltpu.VMEM((ITERS, CHUNKS, *tile), f32),
-            pltpu.VMEM((ITERS, CHUNKS, groups // RADIX, *tile), f32),
-        ]
-        * 2
-        + [pltpu.SemaphoreType.DMA((7,))]
-        + [pltpu.SemaphoreType.DMA((CHUNKS, RADIX))] * 2
-        + [pltpu.SemaphoreType.DMA((groups,))] * 2
-        + [pltpu.SemaphoreType.DMA((CHUNKS, RADIX))] * 2
-        + [pltpu.SemaphoreType.DMA((groups,))] * 2
-        + [pltpu.SemaphoreType.DMA((ITERS, CHUNKS, groups // RADIX))] * 4,
+        + [pltpu.VMEM((ITERS, CHUNKS, *tile), f32)] * 5
+        + [dma((8,))]
+        + [dma((CHUNKS, RADIX))] * 2
+        + [dma((groups,))] * 2
+        + [dma((CHUNKS, RADIX))] * 2
+        + [dma((groups,))] * 2
+        + [dma((CHUNKS + 1,))]
+        + [dma((ITERS, CHUNKS))] * 2
+        + [dma((ITERS, CHUNKS, 2)), dma((ITERS, CHUNKS))],
         compiler_params=pltpu.CompilerParams(
             collective_id=0, has_side_effects=True, vmem_limit_bytes=58 << 20
         ),
-    )(source, conduct, mode_eig, base, shift, *tables)
+    )(source, layer_ids, conduct_table, shift, jnp.asarray(mode_eig), jnp.asarray(eig_y), *tables)
     cells = length_x * length_y * length_z
-    return (result, jnp.sqrt(norms[:ITERS, 0] / cells))
+    back = halves(backward)
+    vmem = pl.BlockSpec(memory_space=pltpu.VMEM)
+    return pl.pallas_call(
+        functools.partial(ending, cells),
+        out_shape=(
+            jax.ShapeDtypeStruct(source.shape, f32),
+            jax.ShapeDtypeStruct((ITERS,), f32),
+        ),
+        in_specs=[hbm] * 3 + [vmem],
+        out_specs=(hbm, smem),
+        scratch_shapes=[
+            pltpu.VMEM(slabs.shape, f32),
+            pltpu.VMEM(back[0].shape, jnp.bfloat16),
+            pltpu.VMEM(back[1].shape, jnp.bfloat16),
+            pltpu.VMEM(source.shape, f32),
+            dma((RADIX, planes + 2)),
+            dma((planes, RADIX)),
+        ],
+        compiler_params=pltpu.CompilerParams(vmem_limit_bytes=32 << 20),
+    )(slabs, *back, sums)
 
 
 def solution(mesh):

time: 85.6 us -> 82.5 us (0.964)
  other arithmetic: 2.94 us -> 0 us
  Pallas kernels: 77 us -> 79.2 us
  local copies, waits for them, and re-layouts: 4.38 us -> 2.31 us
    pallas_call x1 -> x2, Pallas kernels: 77 us -> 79.2 us  [the longest x1 73.1 us: body(): pl.pallas_call(functools.partial(kernel, groups, planes, CHUNKS, layers),...]
    sqrt x1 -> x0, other arithmetic: 1.31 us -> none  [body(): return (result, jnp.sqrt(norms[:ITERS, 0] / cells))]
    unnamed x1 -> x8, local copies, waits for them, and re-layouts: 3.04 us -> 2.31 us
where the time goes in v1:
time: 82.5 us; the launch traced here: 82.2 us
  Pallas kernels  79.2 us (96%)
  local copies, waits for them, and re-layouts  2.31 us (3%)
    pallas_call x1, Pallas kernels, body(): pl.pallas_call(functools.partial(kernel, groups, planes, CHUNKS, layers),...  73.1 us
    pallas_call x1, Pallas kernels, body(): pl.pallas_call(functools.partial(ending, cells), out_shape=(jax.ShapeDtyp...  6.11 us
    unnamed x8, local copies, waits for them, and re-layouts  2.31 us

profile of v1, /device:TPU:1, one launch (start us, length us, event | category | flops | bytes accessed | tf_op | source)
XLA Modules:
  0.0 82.2 jit_solution(6725411460730848338)
XLA Ops:
  0.6 0.0 copy-start.1
  0.6 0.0 copy-start.2
  0.7 73.1 %shard_map.131 = (f32[4,8,2,2,16,256]{5,4,3,2,1,0:T(8,128)}, f32[16,2,128]{2,1,0:T(2,128)}) custom-call(f32[2,2,512,256]{3,2,1,0:T(8,128)} %source_hbm.1, s32[2,256]{1,0:T(2,128)} %ids_hbm.1, f32[16]{0:T(128)} %table.1, f32[2]{0:T(128)} %shift.1, f32[4,8,16,128]{3,2,1,0:T(8,128)} %constant.20.clone.mode_hbm, f32[8,256]{1,0:T(8,128)} %constant.21.clone.eig_hbm, ...), custom_call_target="tpu_custom_call" | custom-call | tf_op jit(solution)/shard_map/pallas_call | solution.py:809
  73.8 0.0 copy-done.1
  73.8 0.0 copy-done.2
  73.8 0.0 copy-start
  73.8 1.6 %copy-done = f32[4,8,2,2,16,256]{5,4,3,2,1,0:T(8,128)S(1)} copy-done((f32[4,8,2,2,16,256]{5,4,3,2,1,0:T(8,128)S(1)}, f32[4,8,2,2,16,256]{5,4,3,2,1,0:T(8,128)}, u32[]{:S(2)}) %copy-start) | copy-done | bytes 2097176
  75.4 0.0 copy-start.3
  75.4 0.7 copy-done.3
  76.1 6.1 %shard_map.132 = (f32[2,2,512,256]{3,2,1,0:T(8,128)}, f32[2]{0:T(128)}) custom-call(f32[4,8,2,2,16,256]{5,4,3,2,1,0:T(8,128)S(1)} %copy-done, bf16[4,256,256]{2,1,0:T(8,128)(2,1)S(1)} %copy-done.2, bf16[4,256,256]{2,1,0:T(8,128)(2,1)S(1)} %copy-done.1, f32[16,2,128]{2,1,0:T(2,128)S(1)} %copy-done.3), custom_call_target="tpu_custom_call" | custom-call | tf_op jit(solution)/shard_map/pallas_call | solution.py:855
Async XLA Ops:
  0.6 73.2 %copy-start.1 = (bf16[4,256,256]{2,1,0:T(8,128)(2,1)S(1)}, bf16[4,256,256]{2,1,0:T(8,128)(2,1)}, u32[]{:S(2)}) copy-start(bf16[4,256,256]{2,1,0:T(8,128)(2,1)} %constant.23.clone.bwd_lo_hbm) | copy-start | bytes 1572868
  0.6 73.2 %copy-start.2 = (bf16[4,256,256]{2,1,0:T(8,128)(2,1)S(1)}, bf16[4,256,256]{2,1,0:T(8,128)(2,1)}, u32[]{:S(2)}) copy-start(bf16[4,256,256]{2,1,0:T(8,128)(2,1)} %constant.22.clone.bwd_hi_hbm) | copy-start | bytes 1572868
  73.8 1.6 %copy-start = (f32[4,8,2,2,16,256]{5,4,3,2,1,0:T(8,128)S(1)}, f32[4,8,2,2,16,256]{5,4,3,2,1,0:T(8,128)}, u32[]{:S(2)}) copy-start(f32[4,8,2,2,16,256]{5,4,3,2,1,0:T(8,128)} %get-tuple-element.4.slabs_hbm) | copy-start | bytes 6291460
  75.4 0.7 copy-start.3

commit v2 on v1

--- a/solution.py
+++ b/solution.py
@@ -194,6 +194,11 @@
 def dot3(left, right):
     mul = functools.partial(jnp.dot, preferred_element_type=jnp.float32)
     return mul(left[0], right[0]) + (mul(left[0], right[1]) + mul(left[1], right[0]))
+
+
+def dot_wide(left, right):
+    wide = jnp.concatenate([left[0], left[1], left[0]], axis=1)
+    return jnp.dot(wide, right, preferred_element_type=jnp.float32)
 
 
 def turn(re, im, quarter):
@@ -524,18 +529,18 @@
                 now = factor(index * depth + level + 1, state[:2])
                 return (*now, *times(now, state[2:]))
 
-            state = lax.fori_loop(0, depth, inner_level, (*carry, one, none))
+            state = lax.fori_loop(0, depth, inner_level, (*carry, one, none), unroll=True)
             put(lines, state[2:], chunk, index)
             return state[:2]
 
         put(alpha, (none, none), chunk, 0)
         lax.fori_loop(0, teams, segment, (none, none))
 
-    sine = (sine_hi[...], sine_lo[...])
+    sine = jnp.concatenate([sine_hi[...], sine_hi[...], sine_lo[...]], axis=0)
 
     def sine_rows(values):
         flat = values.reshape(values.shape[0] * 2 * modes, length_y)
-        return dot3(split(flat), sine).reshape(values.shape)
+        return dot_wide(split(flat), sine).reshape(values.shape)
 
     def launch(turn_id, chunk):
         def rise(index, carry):
@@ -549,7 +554,7 @@
             )
             return (*up, *down)
 
-        ends = lax.fori_loop(0, depth, rise, (none, none, none, none))
+        ends = lax.fori_loop(0, depth, rise, (none, none, none, none), unroll=True)
         put(pair_out, choose(even, ends[:2], ends[2:]), turn_id, chunk)
         pair_copy(turn_id, chunk).start()
         put(rest_out, choose(even, ends[2:], ends[:2]), turn_id, chunk)
@@ -580,7 +585,7 @@
             put(work, now, chunk, index)
             return now
 
-        reached = lax.fori_loop(0, depth, ahead, below)
+        reached = lax.fori_loop(0, depth, ahead, below, unroll=True)
         factor = pair(alpha, chunk, first_level + depth)
         edge = pair(alpha, chunk, last_level)
         echo = times(factor, edge)
@@ -598,7 +603,7 @@
             put(work, now, chunk, index)
             return now
 
-        bottom = lax.fori_loop(0, depth, behind, outer)
+        bottom = lax.fori_loop(0, depth, behind, outer, unroll=True)
         put(work, plus(below, times(pair(alpha, chunk, first_level), bottom)), chunk, depth)
 
     def blocks(values):
@@ -628,7 +633,7 @@
                 rest_sum = rest_sum + rest * rest
             return (given_sum, rest_sum)
 
-        given_sum, rest_sum = lax.fori_loop(0, depth, run, (none, none))
+        given_sum, rest_sum = lax.fori_loop(0, depth, run, (none, none), unroll=4)
         squares[0] = squares[0] + given_sum
         squares[1] = squares[1] + rest_sum
 
@@ -636,50 +641,23 @@
     squares[1] = none
     factors(0)
 
-    def step(index, carry):
-        @pl.when(index < chunks)
-        def _():
-            chunk = index
-            for offset in range(1, RADIX):
-                in_copy(chunk, offset).wait()
-            work[chunk, pl.ds(0, depth)] = sine_rows(forcing[chunk])
-            launch(0, chunk)
-
-        def at(lag, act):
-            @pl.when((index >= lag) & (index < chunks + lag))
-            def _():
-                act(index - lag)
-
-        at(LAGS[0], functools.partial(relay, 0))
-        at(LAGS[2], functools.partial(relay, 1))
-
-        def finish(chunk):
-            solve(1, chunk)
-            values = sine_rows(work[chunk, pl.ds(0, depth)]) * scale
-            result[chunk] = field[chunk, pl.ds(1, depth)] + values
-            for offset in (2, 3, 1):
-                out_copy(chunk, offset).start()
-            own_copy(chunk).start()
-
-        at(LAGS[3], finish)
-
-        def middle(chunk):
-            solve(0, chunk)
-            values = sine_rows(work[chunk]) * scale
-            field[chunk, pl.ds(1, depth)] = values[:depth]
-            field[chunk, 0] = values[depth]
-            field[chunk, depth + 1] = values[depth + 1]
-            residual(chunk)
-            work[chunk, pl.ds(0, depth)] = sine_rows(work[chunk, pl.ds(0, depth)])
-            launch(1, chunk)
-
-        at(LAGS[1], middle)
-
-        @pl.when(index + 1 < chunks)
-        def _():
-            factors(index + 1)
-
-        @pl.when(index == chunks - 1 + LAGS[1])
+    def begin(chunk):
+        for offset in range(1, RADIX):
+            in_copy(chunk, offset).wait()
+        work[chunk, pl.ds(0, depth)] = sine_rows(forcing[chunk])
+        launch(0, chunk)
+
+    def middle(chunk):
+        solve(0, chunk)
+        values = sine_rows(work[chunk]) * scale
+        field[chunk, pl.ds(1, depth)] = values[:depth]
+        field[chunk, 0] = values[depth]
+        field[chunk, depth + 1] = values[depth + 1]
+        residual(chunk)
+        work[chunk, pl.ds(0, depth)] = sine_rows(work[chunk, pl.ds(0, depth)])
+        launch(1, chunk)
+
+        @pl.when(chunk == chunks - 1)
         def _():
             row = lax.broadcasted_iota(jnp.int32, (ITERS, 128), 0)
             both = jnp.where(row == 0, jnp.sum(squares[0]), jnp.sum(squares[1]))
@@ -691,6 +669,36 @@
 
             pltpu.make_async_copy(sum_own, sums.at[me], own_sem.at[chunks]).start()
 
+    def finish(chunk):
+        solve(1, chunk)
+        values = sine_rows(work[chunk, pl.ds(0, depth)]) * scale
+        result[chunk] = field[chunk, pl.ds(1, depth)] + values
+        for offset in (2, 3, 1):
+            out_copy(chunk, offset).start()
+        own_copy(chunk).start()
+
+    def ready(chunk):
+        @pl.when(chunk + 1 < chunks)
+        def _():
+            factors(chunk + 1)
+
+    stages = {
+        "begin": (0, begin),
+        "ready": (0, ready),
+        "relay": (LAGS[0], functools.partial(relay, 0)),
+        "middle": (LAGS[1], middle),
+        "again": (LAGS[2], functools.partial(relay, 1)),
+        "finish": (LAGS[3], finish),
+    }
+
+    def step(index, carry):
+        for name in ORDER:
+            lag, act = stages[name]
+
+            @pl.when((index >= lag) & (index < chunks + lag))
+            def _():
+                act(index - lag)
+
         return carry
 
     lax.fori_loop(0, chunks + LAGS[3], step, 0)
@@ -719,7 +727,7 @@
 
 
 def ending(
-    cells, slabs_hbm, bwd_hi_hbm, bwd_lo_hbm, sums, out, norms, slabs, bwd_hi, bwd_lo, stage, sem, out_sem
+    cells, slabs_hbm, sums_hbm, bwd_hi, bwd_lo, out, norms, slabs, sums, stage, sem, sum_sem, out_sem
 ):
     chunks, planes, _, modes, length_y = slabs.shape[1:]
     count = chunks * modes
@@ -729,20 +737,11 @@
             slabs_hbm.at[residue, :, plane], slabs.at[residue, :, plane], sem.at[residue, plane]
         )
 
-    tables = [
-        [
-            pltpu.make_async_copy(src.at[residue], dst.at[residue], sem.at[residue, planes + index])
-            for index, (src, dst) in enumerate([(bwd_hi_hbm, bwd_hi), (bwd_lo_hbm, bwd_lo)])
-        ]
-        for residue in range(RADIX)
-    ]
-    for residue in range(RADIX):
-        load(residue, 0).start()
-        for table in tables[residue]:
-            table.start()
-    for plane in range(1, planes):
+    for plane in range(planes):
         for residue in range(RADIX):
             load(residue, plane).start()
+    total = pltpu.make_async_copy(sums_hbm, sums, sum_sem)
+    total.start()
 
     def store(plane, q):
         return pltpu.make_async_copy(
@@ -755,9 +754,6 @@
         parts = []
         for residue in range(RADIX):
             load(residue, plane).wait()
-            if plane == 0:
-                for table in tables[residue]:
-                    table.wait()
             blocks = [
                 slabs[residue, chunk, plane, part] for part in range(2) for chunk in range(chunks)
             ]
@@ -769,16 +765,18 @@
             stage[0, plane, q * count : (q + 1) * count, :] = re
             stage[1, plane, q * count : (q + 1) * count, :] = im
             store(plane, q).start()
-    total = jnp.sqrt(jnp.sum(sums[...], axis=0) / cells)
+    total.wait()
+    root = jnp.sqrt(jnp.sum(sums[...], axis=0) / cells)
     for index in range(ITERS):
-        norms[index] = total[index, 0]
+        norms[index] = root[index, 0]
     for plane in range(planes):
         for q in range(RADIX):
             store(plane, q).wait()
 
 
 CHUNKS = 8
-LAGS = (1, 3, 4, 6)
+LAGS = (1, 2, 3, 5)
+ORDER = ("begin", "relay", "finish", "middle", "ready", "again")
 
 
 def body(source, layer_ids, conduct_table, shift):
@@ -858,18 +856,18 @@
             jax.ShapeDtypeStruct(source.shape, f32),
             jax.ShapeDtypeStruct((ITERS,), f32),
         ),
-        in_specs=[hbm] * 3 + [vmem],
+        in_specs=[pl.BlockSpec(memory_space=pltpu.HBM)] * 2 + [vmem] * 2,
         out_specs=(hbm, smem),
         scratch_shapes=[
             pltpu.VMEM(slabs.shape, f32),
-            pltpu.VMEM(back[0].shape, jnp.bfloat16),
-            pltpu.VMEM(back[1].shape, jnp.bfloat16),
+            pltpu.VMEM(sums.shape, f32),
             pltpu.VMEM(source.shape, f32),
-            dma((RADIX, planes + 2)),
+            dma((RADIX, planes)),
+            dma,
             dma((planes, RADIX)),
         ],
-        compiler_params=pltpu.CompilerParams(vmem_limit_bytes=32 << 20),
-    )(slabs, *back, sums)
+        compiler_params=pltpu.CompilerParams(vmem_limit_bytes=62 << 20),
+    )(slabs, sums, *back)
 
 
 def solution(mesh):

time: 82.5 us -> 63.5 us (0.77)
  Pallas kernels: 79.2 us -> 62.5 us
  local copies, waits for them, and re-layouts: 2.31 us -> 0 us
    pallas_call x1, Pallas kernels: 73.1 us -> 55.8 us  [body(): pl.pallas_call(functools.partial(kernel, groups, planes, CHUNKS, layers),...]
    unnamed x8 -> x0, local copies, waits for them, and re-layouts: 2.31 us -> none
where the time goes in v2:
time: 63.5 us; the launch traced here: 63.2 us
  Pallas kernels  62.5 us (98%)
  between operations  0.64 us (1%)
    pallas_call x1, Pallas kernels, body(): pl.pallas_call(functools.partial(kernel, groups, planes, CHUNKS, layers),...  55.8 us
    pallas_call x1, Pallas kernels, body(): pl.pallas_call(functools.partial(ending, cells), out_shape=(jax.ShapeDtyp...  6.68 us

profile of v2, /device:TPU:1, one launch (start us, length us, event | category | flops | bytes accessed | tf_op | source)
XLA Modules:
  0.0 63.2 jit_solution(9344771983740728849)
XLA Ops:
  0.6 55.8 %shard_map.131 = (f32[4,8,2,2,16,256]{5,4,3,2,1,0:T(8,128)}, f32[16,2,128]{2,1,0:T(2,128)}) custom-call(f32[2,2,512,256]{3,2,1,0:T(8,128)} %source_hbm.1, s32[2,256]{1,0:T(2,128)} %ids_hbm.1, f32[16]{0:T(128)} %table.1, f32[2]{0:T(128)} %shift.1, f32[4,8,16,128]{3,2,1,0:T(8,128)} %constant.20.clone.mode_hbm, f32[8,256]{1,0:T(8,128)} %constant.21.clone.eig_hbm, ...), custom_call_target="tpu_custom_call" | custom-call | tf_op jit(solution)/shard_map/pallas_call | solution.py:807
  56.5 6.7 %shard_map.132 = (f32[2,2,512,256]{3,2,1,0:T(8,128)}, f32[2]{0:T(128)}) custom-call(f32[4,8,2,2,16,256]{5,4,3,2,1,0:T(8,128)} %get-tuple-element.4.slabs_hbm, f32[16,2,128]{2,1,0:T(2,128)} %get-tuple-element.5.sums_hbm, bf16[4,256,256]{2,1,0:T(8,128)(2,1)} %constant.22.clone.bwd_hi, bf16[4,256,256]{2,1,0:T(8,128)(2,1)} %constant.23.clone.bwd_lo), custom_call_target="tpu_custom_call" | custom-call | tf_op jit(solution)/shard_map/pallas_call | solution.py:853

commit v3 on v2

--- a/solution.py
+++ b/solution.py
@@ -242,8 +242,8 @@
     layers,
     source_hbm,
     ids_hbm,
-    table,
-    shift,
+    table_hbm,
+    shift_hbm,
     mode_hbm,
     eig_hbm,
     fwd_hi_hbm,
@@ -254,6 +254,8 @@
     sums,
     source,
     ids,
+    table,
+    shift,
     mode_eig,
     eig_y,
     fwd_hi,
@@ -318,10 +320,12 @@
                 (eig_hbm, eig_y),
                 (sine_hi_hbm, sine_hi),
                 (sine_lo_hbm, sine_lo),
+                (table_hbm, table),
+                (shift_hbm, shift),
             ]
         )
     ]
-    for load in [loads[3], *loads[:3], *loads[4:]]:
+    for load in [loads[3], *loads[8:], *loads[:3], *loads[4:8]]:
         load.start()
 
     def remote(src, dst, send, recv, target):
@@ -418,6 +422,8 @@
         )
 
     loads[3].wait()
+    loads[8].wait()
+    loads[9].wait()
     found = jnp.zeros((planes, length_y), jnp.float32)
     for layer in range(layers):
         found = found + jnp.where(ids[...] == layer, table[layer], 0.0)
@@ -463,7 +469,7 @@
         return carry
 
     lax.fori_loop(0, chunks, keep, 0)
-    for load in loads[4:]:
+    for load in loads[4:8]:
         load.wait()
 
     @each_peer
@@ -726,22 +732,9 @@
     lax.fori_loop(0, chunks, settle, 0)
 
 
-def ending(
-    cells, slabs_hbm, sums_hbm, bwd_hi, bwd_lo, out, norms, slabs, sums, stage, sem, sum_sem, out_sem
-):
+def ending(cells, slabs, sums, bwd_hi, bwd_lo, out, norms, stage, out_sem):
     chunks, planes, _, modes, length_y = slabs.shape[1:]
     count = chunks * modes
-
-    def load(residue, plane):
-        return pltpu.make_async_copy(
-            slabs_hbm.at[residue, :, plane], slabs.at[residue, :, plane], sem.at[residue, plane]
-        )
-
-    for plane in range(planes):
-        for residue in range(RADIX):
-            load(residue, plane).start()
-    total = pltpu.make_async_copy(sums_hbm, sums, sum_sem)
-    total.start()
 
     def store(plane, q):
         return pltpu.make_async_copy(
@@ -753,7 +746,6 @@
     for plane in range(planes):
         parts = []
         for residue in range(RADIX):
-            load(residue, plane).wait()
             blocks = [
                 slabs[residue, chunk, plane, part] for part in range(2) for chunk in range(chunks)
             ]
@@ -765,7 +757,6 @@
             stage[0, plane, q * count : (q + 1) * count, :] = re
             stage[1, plane, q * count : (q + 1) * count, :] = im
             store(plane, q).start()
-    total.wait()
     root = jnp.sqrt(jnp.sum(sums[...], axis=0) / cells)
     for index in range(ITERS):
         norms[index] = root[index, 0]
@@ -804,17 +795,20 @@
     hbm = pl.BlockSpec(memory_space=pl.ANY)
     f32 = jnp.float32
     dma = pltpu.SemaphoreType.DMA
+    in_hbm = functools.partial(pltpu.with_memory_space_constraint, memory_space=pltpu.HBM)
     slabs, sums = pl.pallas_call(
         functools.partial(kernel, groups, planes, CHUNKS, layers),
         out_shape=(
-            jax.ShapeDtypeStruct((RADIX, CHUNKS, planes, *tile), f32),
-            jax.ShapeDtypeStruct((groups, ITERS, 128), f32),
+            pltpu.VMEM((RADIX, CHUNKS, planes, *tile), f32),
+            pltpu.VMEM((groups, ITERS, 128), f32),
         ),
-        in_specs=[hbm] * 2 + [smem] * 2 + [hbm] * 6,
+        in_specs=[hbm] * 10,
         out_specs=(hbm, hbm),
         scratch_shapes=[
             pltpu.VMEM(source.shape, f32),
             pltpu.VMEM(layer_ids.shape, jnp.int32),
+            pltpu.SMEM(conduct_table.shape, f32),
+            pltpu.SMEM(shift.shape, f32),
             pltpu.VMEM((CHUNKS, modes, 128), f32),
             pltpu.VMEM((8, length_y), f32),
         ]
@@ -835,7 +829,7 @@
             pltpu.VMEM(tile, f32),
         ]
         + [pltpu.VMEM((ITERS, CHUNKS, *tile), f32)] * 5
-        + [dma((8,))]
+        + [dma((10,))]
         + [dma((CHUNKS, RADIX))] * 2
         + [dma((groups,))] * 2
         + [dma((CHUNKS, RADIX))] * 2
@@ -844,9 +838,15 @@
         + [dma((ITERS, CHUNKS))] * 2
         + [dma((ITERS, CHUNKS, 2)), dma((ITERS, CHUNKS))],
         compiler_params=pltpu.CompilerParams(
-            collective_id=0, has_side_effects=True, vmem_limit_bytes=58 << 20
+            collective_id=0, has_side_effects=True, vmem_limit_bytes=50 << 20
         ),
-    )(source, layer_ids, conduct_table, shift, jnp.asarray(mode_eig), jnp.asarray(eig_y), *tables)
+    )(
+        in_hbm(source),
+        in_hbm(layer_ids),
+        in_hbm(conduct_table),
+        in_hbm(shift),
+        *[in_hbm(jnp.asarray(table)) for table in (mode_eig, eig_y, *tables)],
+    )
     cells = length_x * length_y * length_z
     back = halves(backward)
     vmem = pl.BlockSpec(memory_space=pltpu.VMEM)
@@ -856,17 +856,10 @@
             jax.ShapeDtypeStruct(source.shape, f32),
             jax.ShapeDtypeStruct((ITERS,), f32),
         ),
-        in_specs=[pl.BlockSpec(memory_space=pltpu.HBM)] * 2 + [vmem] * 2,
+        in_specs=[vmem] * 4,
         out_specs=(hbm, smem),
-        scratch_shapes=[
-            pltpu.VMEM(slabs.shape, f32),
-            pltpu.VMEM(sums.shape, f32),
-            pltpu.VMEM(source.shape, f32),
-            dma((RADIX, planes)),
-            dma,
-            dma((planes, RADIX)),
-        ],
-        compiler_params=pltpu.CompilerParams(vmem_limit_bytes=62 << 20),
+        scratch_shapes=[pltpu.VMEM(source.shape, f32), dma((planes, RADIX))],
+        compiler_params=pltpu.CompilerParams(vmem_limit_bytes=20 << 20),
     )(slabs, sums, *back)
 
 

time: 63.5 us -> 58.7 us (0.924)
  Pallas kernels: 62.5 us -> 57.8 us
    pallas_call x1, Pallas kernels: 6.68 us -> 2.75 us  [body(): pl.pallas_call(functools.partial(ending, cells), out_shape=(jax.ShapeDtyp...]
    pallas_call x1, Pallas kernels: 55.8 us -> 55.1 us  [body(): pl.pallas_call(functools.partial(kernel, groups, planes, CHUNKS, layers),...]
where the time goes in v3:
time: 58.7 us; the launch traced here: 58.5 us
  Pallas kernels  57.8 us (98%)
  between operations  0.67 us (1%)
    pallas_call x1, Pallas kernels, body(): pl.pallas_call(functools.partial(kernel, groups, planes, CHUNKS, layers),...  55.1 us
    pallas_call x1, Pallas kernels, body(): pl.pallas_call(functools.partial(ending, cells), out_shape=(jax.ShapeDtyp...  2.75 us

profile of v3, /device:TPU:1, one launch (start us, length us, event | category | flops | bytes accessed | tf_op | source)
XLA Modules:
  0.0 58.5 jit_solution(16464710540080775857)
XLA Ops:
  0.6 0.0 copy-start
  0.6 0.0 copy-start.1
  0.7 55.1 %shard_map.131 = (f32[4,8,2,2,16,256]{5,4,3,2,1,0:T(8,128)S(1)}, f32[16,2,128]{2,1,0:T(2,128)S(1)}) custom-call(f32[2,2,512,256]{3,2,1,0:T(8,128)} %source_hbm.1, s32[2,256]{1,0:T(2,128)} %ids_hbm.1, f32[16]{0:T(128)} %table_hbm.1, f32[2]{0:T(128)} %shift_hbm.1, f32[4,8,16,128]{3,2,1,0:T(8,128)} %constant.20.clone.mode_hbm, ...), custom_call_target="tpu_custom_call" | custom-call | tf_op jit(solution)/shard_map/pallas_call | solution.py:799
  55.7 0.0 copy-done
  55.7 0.0 copy-done.1
  55.8 2.7 %shard_map.132 = (f32[2,2,512,256]{3,2,1,0:T(8,128)}, f32[2]{0:T(128)}) custom-call(f32[4,8,2,2,16,256]{5,4,3,2,1,0:T(8,128)S(1)} %get-tuple-element.4.slabs, f32[16,2,128]{2,1,0:T(2,128)S(1)} %get-tuple-element.5.sums, bf16[4,256,256]{2,1,0:T(8,128)(2,1)S(1)} %copy-done.1, bf16[4,256,256]{2,1,0:T(8,128)(2,1)S(1)} %copy-done), custom_call_target="tpu_custom_call" | custom-call | tf_op jit(solution)/shard_map/pallas_call | solution.py:853
Async XLA Ops:
  0.6 55.1 %copy-start = (bf16[4,256,256]{2,1,0:T(8,128)(2,1)S(1)}, bf16[4,256,256]{2,1,0:T(8,128)(2,1)}, u32[]{:S(2)}) copy-start(bf16[4,256,256]{2,1,0:T(8,128)(2,1)} %constant.23.clone.bwd_lo) | copy-start | bytes 1572868
  0.6 55.1 %copy-start.1 = (bf16[4,256,256]{2,1,0:T(8,128)(2,1)S(1)}, bf16[4,256,256]{2,1,0:T(8,128)(2,1)}, u32[]{:S(2)}) copy-start(bf16[4,256,256]{2,1,0:T(8,128)(2,1)} %constant.22.clone.bwd_hi) | copy-start | bytes 1572868

commit v4 on v3

--- a/solution.py
+++ b/solution.py
@@ -265,8 +265,12 @@
     spectra,
     forcing,
     cond_own,
-    cond_all,
+    cond_team,
     cond,
+    edge_out,
+    edge_in,
+    half_out,
+    half_in,
     faces,
     work,
     alpha,
@@ -285,6 +289,10 @@
     in_recv,
     cond_send,
     cond_recv,
+    edge_send,
+    edge_recv,
+    half_send,
+    half_recv,
     out_send,
     out_recv,
     sum_send,
@@ -308,24 +316,19 @@
     first_level = team * depth
     last_level = length_z - first_level - depth
 
+    pieces = [(ids_hbm, ids), (table_hbm, table), (shift_hbm, shift)]
+    pieces += [(source_hbm.at[:, 0], source.at[:, 0])]
+    for residue in range(RADIX):
+        pieces += [(fwd_hi_hbm.at[residue], fwd_hi.at[residue])]
+        pieces += [(fwd_lo_hbm.at[residue], fwd_lo.at[residue])]
+    pieces += [(source_hbm.at[:, plane], source.at[:, plane]) for plane in range(1, planes)]
+    pieces += [(sine_hi_hbm, sine_hi), (sine_lo_hbm, sine_lo)]
+    pieces += [(mode_hbm.at[side], mode_eig), (eig_hbm, eig_y)]
     loads = [
         pltpu.make_async_copy(src, dst, load_sem.at[index])
-        for index, (src, dst) in enumerate(
-            [
-                (source_hbm, source),
-                (fwd_hi_hbm, fwd_hi),
-                (fwd_lo_hbm, fwd_lo),
-                (ids_hbm, ids),
-                (mode_hbm.at[side], mode_eig),
-                (eig_hbm, eig_y),
-                (sine_hi_hbm, sine_hi),
-                (sine_lo_hbm, sine_lo),
-                (table_hbm, table),
-                (shift_hbm, shift),
-            ]
-        )
+        for index, (src, dst) in enumerate(pieces)
     ]
-    for load in [loads[3], *loads[8:], *loads[:3], *loads[4:8]]:
+    for load in loads:
         load.start()
 
     def remote(src, dst, send, recv, target):
@@ -349,12 +352,41 @@
 
     def cond_copy(offset):
         return remote(
-            cond_own, cond_all.at[me], cond_send.at[offset], cond_recv.at[offset], peer(offset)
+            cond_own,
+            cond_team.at[side],
+            cond_send.at[offset],
+            cond_recv.at[offset],
+            team * RADIX + mate(offset),
+        )
+
+    def edge_copy(which):
+        return remote(
+            edge_out,
+            edge_in.at[which],
+            edge_send.at[which],
+            edge_recv.at[which],
+            me + [RADIX, -RADIX][which],
+        )
+
+    def half_copy(which):
+        target = [teams - 1 - team, (teams - 1) * (2 - team)][which]
+        return remote(
+            half_out, half_in, half_send.at[which], half_recv.at[0], target * RADIX + side
         )
 
     def sum_copy(offset):
         return remote(
             sum_own, sums.at[me], sum_send.at[offset], sum_recv.at[offset], peer(offset)
+        )
+
+    def in_piece(chunk, offset, plane):
+        target = mate(offset)
+        return remote(
+            spectra.at[target, chunk, pl.ds(plane, 1)],
+            forcing.at[chunk, pl.ds(side * planes + plane, 1)],
+            in_send.at[chunk, offset],
+            in_recv.at[chunk, offset],
+            team * RADIX + target,
         )
 
     def in_copy(chunk, offset):
@@ -415,24 +447,32 @@
 
     barrier = pltpu.get_barrier_semaphore()
 
-    @each_peer
-    def _(offset):
+    def greet(target):
         pl.semaphore_signal(
-            barrier, inc=1, device_id={"gz": peer(offset)}, device_id_type=pl.DeviceIdType.MESH
-        )
-
-    loads[3].wait()
-    loads[8].wait()
-    loads[9].wait()
+            barrier, inc=1, device_id={"gz": target}, device_id_type=pl.DeviceIdType.MESH
+        )
+
+    for offset in range(1, RADIX):
+        greet(team * RADIX + mate(offset))
+
+    @pl.when(team > 0)
+    def _():
+        greet(me - RADIX)
+
+    @pl.when(team < teams - 1)
+    def _():
+        greet(me + RADIX)
+
+    for load in loads[:3]:
+        load.wait()
     found = jnp.zeros((planes, length_y), jnp.float32)
     for layer in range(layers):
         found = found + jnp.where(ids[...] == layer, table[layer], 0.0)
     cond_own[...] = found
-    cond_all[me] = found
-    for load in loads[:3]:
-        load.wait()
-
-    def forward(plane, carry):
+    cond_team[side] = found
+
+    def forward(plane):
+        loads[3 if plane == 0 else 3 + 2 * RADIX + plane].wait()
         parts = [
             (
                 source[0, plane, q * count : (q + 1) * count, :],
@@ -441,6 +481,9 @@
             for q in range(RADIX)
         ]
         for residue in range(RADIX):
+            if plane == 0:
+                loads[4 + 2 * residue].wait()
+                loads[5 + 2 * residue].wait()
             mixed = combine(parts, [-residue * q for q in range(RADIX)])
             right = split(jnp.concatenate(mixed, axis=0))
             values = dot3((fwd_hi[residue], fwd_lo[residue]), right)
@@ -448,64 +491,108 @@
                 for part in range(2):
                     start = part * count + chunk * modes
                     spectra[residue, chunk, plane, part] = values[start : start + modes]
-        return carry
-
-    lax.fori_loop(0, planes, forward, 0)
-    pl.semaphore_wait(barrier, groups - 1)
-
-    @each_peer
-    def _(offset):
+
+    forward(0)
+    pl.semaphore_wait(barrier, RADIX - 1 + jnp.where(team > 0, 1, 0) + jnp.where(team < teams - 1, 1, 0))
+    for offset in range(1, RADIX):
         cond_copy(offset).start()
+    for offset in (2, 3, 1):
+        in_piece(0, offset, 0).start()
+    for plane in range(1, planes):
+        forward(plane)
+        for offset in (2, 3, 1):
+            in_piece(0, offset, plane).start()
+
+    for load in loads[3 + 2 * RADIX + planes :]:
+        load.wait()
+    sine = jnp.concatenate([sine_hi[...], sine_hi[...], sine_lo[...]], axis=0)
+
+    def sine_rows(values):
+        flat = values.reshape(-1, length_y)
+        return dot_wide(split(flat), sine).reshape(values.shape)
 
     def send_in(chunk, carry):
+        spectra[:, chunk] = sine_rows(spectra[:, chunk])
         for offset in (2, 3, 1):
             in_copy(chunk, offset).start()
         return carry
 
-    lax.fori_loop(0, chunks, send_in, 0)
+    lax.fori_loop(1, 2, send_in, 0)
+    for offset in range(1, RADIX):
+        cond_copy(offset).wait()
+    total = jnp.zeros((1, length_y), jnp.float32)
+    for index in range(RADIX):
+        for plane in range(planes):
+            row = cond_team[index, plane : plane + 1, :]
+            cond[index * planes + plane + 1] = jnp.broadcast_to(row, (8, length_y))
+            total = total + row
+    edge_out[0:1] = total
+    edge_out[1:2] = cond_team[0, 0:1, :]
+    edge_out[2:3] = cond_team[RADIX - 1, planes - 1 : planes, :]
+
+    @pl.when(team < teams - 1)
+    def _():
+        edge_copy(0).start()
+
+    @pl.when(team > 0)
+    def _():
+        edge_copy(1).start()
+
+    lax.fori_loop(2, chunks - 3, send_in, 0)
+
+
+    @pl.when(team > 0)
+    def _():
+        edge_copy(0).wait_recv()
+        cond[0] = jnp.broadcast_to(edge_in[0, 2:3, :], (8, length_y))
+
+    @pl.when(team == 0)
+    def _():
+        cond[0] = cond[1]
+
+    @pl.when(team < teams - 1)
+    def _():
+        edge_copy(1).wait_recv()
+        cond[depth + 1] = jnp.broadcast_to(edge_in[1, 1:2, :], (8, length_y))
+
+    @pl.when(team == teams - 1)
+    def _():
+        cond[depth + 1] = cond[depth]
+
+    @pl.when(even)
+    def _():
+        half_out[0:1] = total + edge_in[1, 0:1, :]
+
+    @pl.when(jnp.logical_not(even))
+    def _():
+        half_out[0:1] = total + edge_in[0, 0:1, :]
+
+    @pl.when(inner)
+    def _():
+        half_copy(1).start()
+        half_copy(0).start()
+
+    shift_re = shift[0]
+    shift_im = shift[1]
+    row_lane = lax.broadcasted_iota(jnp.int32, (8, length_y), 1)
+    last = length_y - 1
+
+    lax.fori_loop(chunks - 3, chunks, send_in, 0)
 
     def keep(chunk, carry):
         forcing[chunk, rows(side)] = spectra[side, chunk]
         return carry
 
     lax.fori_loop(0, chunks, keep, 0)
-    for load in loads[4:8]:
-        load.wait()
-
-    @each_peer
-    def _(offset):
-        cond_copy(offset).wait()
-
-    def spread(index, total):
-        for plane in range(planes):
-            row = jnp.broadcast_to(cond_all[index, plane : plane + 1, :], (8, length_y))
-            cond[index * planes + plane + 1] = row
-            total = total + row
-        return total
-
-    total = lax.fori_loop(0, groups, spread, jnp.zeros((8, length_y), jnp.float32))
-    cond[0] = cond[1]
-    cond[length_z + 1] = cond[length_z]
-    mean_cond = jnp.sum(total) / (8 * length_y * length_z)
-    shift_re = shift[0]
-    shift_im = shift[1]
-    scale = relax / mean_cond
-    offset_re = shift_re / mean_cond
-    diag_im = shift_im / mean_cond
-    none = jnp.zeros((modes, length_y), jnp.float32)
-    one = jnp.ones((modes, length_y), jnp.float32)
-    row_lane = lax.broadcasted_iota(jnp.int32, (8, length_y), 1)
-    last = length_y - 1
 
     def make_faces(index, carry):
-        level = first_level + index
-        here = cond[level + 1]
+        here = cond[index + 1]
         right = jnp.where(row_lane == last, here, pltpu.roll(here, last, 1))
         left = jnp.where(row_lane == 0, here, pltpu.roll(here, 1, 1))
         face_yp = 0.5 * (here + right)
         face_ym = 0.5 * (here + left)
-        face_zp = 0.5 * (here + cond[level + 2])
-        face_zm = 0.5 * (here + cond[level])
+        face_zp = 0.5 * (here + cond[index + 2])
+        face_zm = 0.5 * (here + cond[index])
         faces[index, 0] = here
         faces[index, 1] = face_yp + face_ym + face_zp + face_zm + shift_re
         faces[index, 2] = jnp.where(row_lane == last, 0.0, face_yp)
@@ -515,6 +602,20 @@
         return carry
 
     lax.fori_loop(0, depth, make_faces, 0)
+    def take(chunk):
+        for offset in range(1, RADIX):
+            in_copy(chunk, offset).wait()
+
+    take(0)
+    forcing[0] = sine_rows(forcing[0])
+    half_copy(0).wait_recv()
+    total = half_out[0:1, :] + half_in[0:1, :]
+    mean_cond = jnp.sum(total) / (length_y * length_z)
+    scale = relax / mean_cond
+    offset_re = shift_re / mean_cond
+    diag_im = shift_im / mean_cond
+    none = jnp.zeros((modes, length_y), jnp.float32)
+    one = jnp.ones((modes, length_y), jnp.float32)
 
     def eigen(chunk):
         return jnp.concatenate([mode_eig[chunk]] * (length_y // 128), axis=1)
@@ -542,21 +643,17 @@
         put(alpha, (none, none), chunk, 0)
         lax.fori_loop(0, teams, segment, (none, none))
 
-    sine = jnp.concatenate([sine_hi[...], sine_hi[...], sine_lo[...]], axis=0)
-
-    def sine_rows(values):
-        flat = values.reshape(values.shape[0] * 2 * modes, length_y)
-        return dot_wide(split(flat), sine).reshape(values.shape)
+    given = (forcing, work)
 
     def launch(turn_id, chunk):
         def rise(index, carry):
             up = times(
                 pair(alpha, chunk, first_level + index + 1),
-                plus(pair(work, chunk, index), carry[:2]),
+                plus(pair(given[turn_id], chunk, index), carry[:2]),
             )
             down = times(
                 pair(alpha, chunk, last_level + index + 1),
-                plus(pair(work, chunk, depth - 1 - index), carry[2:]),
+                plus(pair(given[turn_id], chunk, depth - 1 - index), carry[2:]),
             )
             return (*up, *down)
 
@@ -587,7 +684,7 @@
 
         def ahead(index, carry):
             factor = pair(alpha, chunk, first_level + index + 1)
-            now = times(factor, plus(pair(work, chunk, index), carry))
+            now = times(factor, plus(pair(given[turn_id], chunk, index), carry))
             put(work, now, chunk, index)
             return now
 
@@ -615,11 +712,10 @@
     def blocks(values):
         return values.reshape(modes // 8, 8, length_y)
 
-    def residual(chunk):
+    def operator(chunk):
         eig = blocks(eigen(chunk))
 
         def run(index, carry):
-            given_sum, rest_sum = carry
             center = faces[index, 0] * eig + faces[index, 1]
             values = pair(field, chunk, index + 1)
             turned = (-shift_im * values[1], shift_im * values[0])
@@ -632,25 +728,20 @@
                 applied = applied - faces[index, 3] * blocks(pltpu.roll(value, 1, 1))
                 applied = applied - faces[index, 4] * blocks(above[part])
                 applied = applied - faces[index, 5] * blocks(below[part])
-                given = forcing[chunk, index, part]
-                rest = given - applied.reshape(modes, length_y)
-                work[chunk, index, part] = rest
-                given_sum = given_sum + given * given
-                rest_sum = rest_sum + rest * rest
-            return (given_sum, rest_sum)
-
-        given_sum, rest_sum = lax.fori_loop(0, depth, run, (none, none), unroll=4)
-        squares[0] = squares[0] + given_sum
-        squares[1] = squares[1] + rest_sum
+                work[chunk, index, part] = applied.reshape(modes, length_y)
+            return carry
+
+        lax.fori_loop(0, depth, run, 0, unroll=8)
 
     squares[0] = none
     squares[1] = none
     factors(0)
 
     def begin(chunk):
-        for offset in range(1, RADIX):
-            in_copy(chunk, offset).wait()
-        work[chunk, pl.ds(0, depth)] = sine_rows(forcing[chunk])
+        @pl.when(chunk > 0)
+        def _():
+            take(chunk)
+
         launch(0, chunk)
 
     def middle(chunk):
@@ -659,9 +750,13 @@
         field[chunk, pl.ds(1, depth)] = values[:depth]
         field[chunk, 0] = values[depth]
         field[chunk, depth + 1] = values[depth + 1]
-        residual(chunk)
-        work[chunk, pl.ds(0, depth)] = sine_rows(work[chunk, pl.ds(0, depth)])
+        operator(chunk)
+        here = forcing[chunk]
+        rest = here - sine_rows(work[chunk, pl.ds(0, depth)])
+        work[chunk, pl.ds(0, depth)] = rest
         launch(1, chunk)
+        squares[0] = squares[0] + jnp.sum(here * here, axis=(0, 1))
+        squares[1] = squares[1] + jnp.sum(rest * rest, axis=(0, 1))
 
         @pl.when(chunk == chunks - 1)
         def _():
@@ -724,6 +819,19 @@
         return carry
 
     pltpu.make_async_copy(sum_own, sums.at[me], own_sem.at[chunks]).wait()
+
+    @pl.when(team < teams - 1)
+    def _():
+        edge_copy(0).wait_send()
+
+    @pl.when(team > 0)
+    def _():
+        edge_copy(1).wait_send()
+
+    @pl.when(inner)
+    def _():
+        half_copy(0).wait_send()
+        half_copy(1).wait_send()
 
     @each_peer
     def _(offset):
@@ -817,8 +925,12 @@
             pltpu.VMEM((RADIX, CHUNKS, planes, *tile), f32),
             pltpu.VMEM((CHUNKS, depth, *tile), f32),
             pltpu.VMEM((planes, length_y), f32),
-            pltpu.VMEM((groups, planes, length_y), f32),
-            pltpu.VMEM((length_z + 2, 8, length_y), f32),
+            pltpu.VMEM((RADIX, planes, length_y), f32),
+            pltpu.VMEM((depth + 2, 8, length_y), f32),
+            pltpu.VMEM((4, length_y), f32),
+            pltpu.VMEM((2, 4, length_y), f32),
+            pltpu.VMEM((4, length_y), f32),
+            pltpu.VMEM((4, length_y), f32),
             pltpu.VMEM((depth, 6, 8, length_y), f32),
             pltpu.VMEM((CHUNKS, depth + 2, *tile), f32),
             pltpu.VMEM((CHUNKS, length_z + 1, *tile), f32),
@@ -829,9 +941,11 @@
             pltpu.VMEM(tile, f32),
         ]
         + [pltpu.VMEM((ITERS, CHUNKS, *tile), f32)] * 5
-        + [dma((10,))]
+        + [dma((7 + 2 * RADIX + planes,))]
         + [dma((CHUNKS, RADIX))] * 2
-        + [dma((groups,))] * 2
+        + [dma((RADIX,))] * 2
+        + [dma((2,))] * 2
+        + [dma((2,)), dma((1,))]
         + [dma((CHUNKS, RADIX))] * 2
         + [dma((groups,))] * 2
         + [dma((CHUNKS + 1,))]

time: 58.7 us -> 58.1 us (0.990)
  no operation moved by 1% of the time
where the time goes in v4:
time: 58.1 us; the launch traced here: 57.9 us
  Pallas kernels  57.3 us (99%)
  between operations  0.67 us (1%)
    pallas_call x1, Pallas kernels, body(): pl.pallas_call(functools.partial(kernel, groups, planes, CHUNKS, layers),...  54.5 us
    pallas_call x1, Pallas kernels, body(): pl.pallas_call(functools.partial(ending, cells), out_shape=(jax.ShapeDtyp...  2.74 us

profile of v4, /device:TPU:1, one launch (start us, length us, event | category | flops | bytes accessed | tf_op | source)
XLA Modules:
  0.0 57.9 jit_solution(13636390774077699620)
XLA Ops:
  0.6 0.0 copy-start
  0.6 0.0 copy-start.1
  0.7 54.5 %shard_map.131 = (f32[4,8,2,2,16,256]{5,4,3,2,1,0:T(8,128)S(1)}, f32[16,2,128]{2,1,0:T(2,128)S(1)}) custom-call(f32[2,2,512,256]{3,2,1,0:T(8,128)} %source_hbm.1, s32[2,256]{1,0:T(2,128)} %ids_hbm.1, f32[16]{0:T(128)} %table_hbm.1, f32[2]{0:T(128)} %shift_hbm.1, f32[4,8,16,128]{3,2,1,0:T(8,128)} %constant.20.clone.mode_hbm, ...), custom_call_target="tpu_custom_call" | custom-call | tf_op jit(solution)/shard_map/pallas_call | solution.py:907
  55.2 0.0 copy-done
  55.2 0.0 copy-done.1
  55.2 2.7 %shard_map.132 = (f32[2,2,512,256]{3,2,1,0:T(8,128)}, f32[2]{0:T(128)}) custom-call(f32[4,8,2,2,16,256]{5,4,3,2,1,0:T(8,128)S(1)} %get-tuple-element.4.slabs, f32[16,2,128]{2,1,0:T(2,128)S(1)} %get-tuple-element.5.sums, bf16[4,256,256]{2,1,0:T(8,128)(2,1)S(1)} %copy-done.1, bf16[4,256,256]{2,1,0:T(8,128)(2,1)S(1)} %copy-done), custom_call_target="tpu_custom_call" | custom-call | tf_op jit(solution)/shard_map/pallas_call | solution.py:967
Async XLA Ops:
  0.6 54.6 %copy-start = (bf16[4,256,256]{2,1,0:T(8,128)(2,1)S(1)}, bf16[4,256,256]{2,1,0:T(8,128)(2,1)}, u32[]{:S(2)}) copy-start(bf16[4,256,256]{2,1,0:T(8,128)(2,1)} %constant.23.clone.bwd_lo) | copy-start | bytes 1572868
  0.6 54.6 %copy-start.1 = (bf16[4,256,256]{2,1,0:T(8,128)(2,1)S(1)}, bf16[4,256,256]{2,1,0:T(8,128)(2,1)}, u32[]{:S(2)}) copy-start(bf16[4,256,256]{2,1,0:T(8,128)(2,1)} %constant.22.clone.bwd_hi) | copy-start | bytes 1572868

commit v5 on v4

--- a/solution.py
+++ b/solution.py
@@ -250,7 +250,10 @@
     fwd_lo_hbm,
     sine_hi_hbm,
     sine_lo_hbm,
-    slabs,
+    bwd_hi_hbm,
+    bwd_lo_hbm,
+    partial,
+    tail,
     sums,
     source,
     ids,
@@ -262,6 +265,9 @@
     fwd_lo,
     sine_hi,
     sine_lo,
+    bwd_hi,
+    bwd_lo,
+    slabs,
     spectra,
     forcing,
     cond_own,
@@ -324,11 +330,13 @@
     pieces += [(source_hbm.at[:, plane], source.at[:, plane]) for plane in range(1, planes)]
     pieces += [(sine_hi_hbm, sine_hi), (sine_lo_hbm, sine_lo)]
     pieces += [(mode_hbm.at[side], mode_eig), (eig_hbm, eig_y)]
+    later = len(pieces)
+    pieces += [(bwd_hi_hbm, bwd_hi), (bwd_lo_hbm, bwd_lo)]
     loads = [
         pltpu.make_async_copy(src, dst, load_sem.at[index])
         for index, (src, dst) in enumerate(pieces)
     ]
-    for load in loads:
+    for load in loads[:later]:
         load.start()
 
     def remote(src, dst, send, recv, target):
@@ -399,19 +407,24 @@
             team * RADIX + target,
         )
 
+    def landing(chunk):
+        return tail.at[side] if chunk is None else slabs.at[side, chunk]
+
     def out_copy(chunk, offset):
         target = mate(offset)
+        index = chunks - 1 if chunk is None else chunk
         return remote(
-            result.at[chunk, rows(target)],
-            slabs.at[side, chunk],
-            out_send.at[chunk, offset],
-            out_recv.at[chunk, offset],
+            result.at[index, rows(target)],
+            landing(chunk),
+            out_send.at[index, offset],
+            out_recv.at[index, offset],
             team * RADIX + target,
         )
 
     def own_copy(chunk):
+        index = chunks - 1 if chunk is None else chunk
         return pltpu.make_async_copy(
-            result.at[chunk, rows(side)], slabs.at[side, chunk], own_sem.at[chunk]
+            result.at[index, rows(side)], landing(chunk), own_sem.at[index]
         )
 
     even = lax.rem(team, 2) == 0
@@ -492,10 +505,11 @@
                     start = part * count + chunk * modes
                     spectra[residue, chunk, plane, part] = values[start : start + modes]
 
-    forward(0)
-    pl.semaphore_wait(barrier, RADIX - 1 + jnp.where(team > 0, 1, 0) + jnp.where(team < teams - 1, 1, 0))
+    ends = jnp.where((team > 0) & (team < teams - 1), 0, 1)
+    pl.semaphore_wait(barrier, RADIX + 1 - ends)
     for offset in range(1, RADIX):
         cond_copy(offset).start()
+    forward(0)
     for offset in (2, 3, 1):
         in_piece(0, offset, 0).start()
     for plane in range(1, planes):
@@ -503,8 +517,10 @@
         for offset in (2, 3, 1):
             in_piece(0, offset, plane).start()
 
-    for load in loads[3 + 2 * RADIX + planes :]:
+    for load in loads[3 + 2 * RADIX + planes : later]:
         load.wait()
+    for load in loads[later:]:
+        load.start()
     sine = jnp.concatenate([sine_hi[...], sine_hi[...], sine_lo[...]], axis=0)
 
     def sine_rows(values):
@@ -774,9 +790,19 @@
         solve(1, chunk)
         values = sine_rows(work[chunk, pl.ds(0, depth)]) * scale
         result[chunk] = field[chunk, pl.ds(1, depth)] + values
-        for offset in (2, 3, 1):
-            out_copy(chunk, offset).start()
-        own_copy(chunk).start()
+
+        def put_out(which):
+            for offset in (2, 3, 1):
+                out_copy(which, offset).start()
+            own_copy(which).start()
+
+        @pl.when(chunk < chunks - 1)
+        def _():
+            put_out(chunk)
+
+        @pl.when(chunk == chunks - 1)
+        def _():
+            put_out(None)
 
     def ready(chunk):
         @pl.when(chunk + 1 < chunks)
@@ -813,11 +839,30 @@
                 comb_copy(turn_id, chunk, 0).wait_send()
                 comb_copy(turn_id, chunk, 1).wait_send()
 
+        return carry
+
+    def arrive(chunk, carry):
         own_copy(chunk).wait()
         for offset in range(1, RADIX):
             out_copy(chunk, offset).wait()
         return carry
 
+    for load in loads[later:]:
+        load.wait()
+    lax.fori_loop(0, chunks - 1, arrive, 0)
+
+    def gather(plane, carry):
+        for residue in range(RADIX):
+            blocks = []
+            for part in range(2):
+                blocks += [slabs[residue, chunk, plane, part] for chunk in range(chunks - 1)]
+                blocks += [none]
+            right = split(jnp.concatenate(blocks, axis=0))
+            partial[plane, residue] = dot3((bwd_hi[residue], bwd_lo[residue]), right)
+        return carry
+
+    lax.fori_loop(0, planes, gather, 0)
+
     pltpu.make_async_copy(sum_own, sums.at[me], own_sem.at[chunks]).wait()
 
     @pl.when(team < teams - 1)
@@ -838,11 +883,13 @@
         sum_copy(offset).wait()
 
     lax.fori_loop(0, chunks, settle, 0)
-
-
-def ending(cells, slabs, sums, bwd_hi, bwd_lo, out, norms, stage, out_sem):
-    chunks, planes, _, modes, length_y = slabs.shape[1:]
-    count = chunks * modes
+    arrive(None, 0)
+
+
+def ending(cells, partial, tail, sums, table, out, norms, stage, out_sem):
+    planes, _, twice, length_y = partial.shape
+    count = twice // 2
+    modes = tail.shape[3]
 
     def store(plane, q):
         return pltpu.make_async_copy(
@@ -854,11 +901,10 @@
     for plane in range(planes):
         parts = []
         for residue in range(RADIX):
-            blocks = [
-                slabs[residue, chunk, plane, part] for part in range(2) for chunk in range(chunks)
-            ]
-            right = split(jnp.concatenate(blocks, axis=0))
-            values = dot3((bwd_hi[residue], bwd_lo[residue]), right)
+            high, low = split(tail[residue, plane].reshape(2 * modes, length_y))
+            right = jnp.concatenate([high, low, high], axis=0)
+            more = jnp.dot(table[residue], right, preferred_element_type=jnp.float32)
+            values = partial[plane, residue] + more
             parts.append((values[:count], values[count:]))
         for q in range(RADIX):
             re, im = combine(parts, [residue * q for residue in range(RADIX)])
@@ -897,21 +943,28 @@
     eig_y = 4.0 - 2.0 * np.cos(np.pi / (length_y + 1) * (np.arange(length_y) + 1.0))
     eig_y = np.ascontiguousarray(np.broadcast_to(eig_y.astype(np.float32), (8, length_y)))
     forward, backward = radix_tables(length_x)
-    tables = [*halves(forward), *halves(sine_host(length_y))]
+    tables = [*halves(forward), *halves(sine_host(length_y)), *halves(backward)]
+    final = np.concatenate([part * count + np.arange(count - modes, count) for part in range(2)])
+    final = backward[:, :, final]
+    high = final.astype(jnp.bfloat16)
+    low = (final - high.astype(np.float32)).astype(jnp.bfloat16)
+    final = jnp.asarray(np.concatenate([high, high, low], axis=2))
     tile = (2, modes, length_y)
     smem = pl.BlockSpec(memory_space=pltpu.SMEM)
     hbm = pl.BlockSpec(memory_space=pl.ANY)
+    vmem = pl.BlockSpec(memory_space=pltpu.VMEM)
     f32 = jnp.float32
     dma = pltpu.SemaphoreType.DMA
     in_hbm = functools.partial(pltpu.with_memory_space_constraint, memory_space=pltpu.HBM)
-    slabs, sums = pl.pallas_call(
+    partial, tail, sums = pl.pallas_call(
         functools.partial(kernel, groups, planes, CHUNKS, layers),
         out_shape=(
-            pltpu.VMEM((RADIX, CHUNKS, planes, *tile), f32),
+            pltpu.VMEM((planes, RADIX, 2 * count, length_y), f32),
+            pltpu.VMEM((RADIX, planes, *tile), f32),
             pltpu.VMEM((groups, ITERS, 128), f32),
         ),
-        in_specs=[hbm] * 10,
-        out_specs=(hbm, hbm),
+        in_specs=[hbm] * 12,
+        out_specs=(vmem, hbm, hbm),
         scratch_shapes=[
             pltpu.VMEM(source.shape, f32),
             pltpu.VMEM(layer_ids.shape, jnp.int32),
@@ -922,6 +975,7 @@
         ]
         + [pltpu.VMEM(table.shape, jnp.bfloat16) for table in tables]
         + [
+            pltpu.VMEM((RADIX, CHUNKS - 1, planes, *tile), f32),
             pltpu.VMEM((RADIX, CHUNKS, planes, *tile), f32),
             pltpu.VMEM((CHUNKS, depth, *tile), f32),
             pltpu.VMEM((planes, length_y), f32),
@@ -941,7 +995,7 @@
             pltpu.VMEM(tile, f32),
         ]
         + [pltpu.VMEM((ITERS, CHUNKS, *tile), f32)] * 5
-        + [dma((7 + 2 * RADIX + planes,))]
+        + [dma((9 + 2 * RADIX + planes,))]
         + [dma((CHUNKS, RADIX))] * 2
         + [dma((RADIX,))] * 2
         + [dma((2,))] * 2
@@ -962,8 +1016,6 @@
         *[in_hbm(jnp.asarray(table)) for table in (mode_eig, eig_y, *tables)],
     )
     cells = length_x * length_y * length_z
-    back = halves(backward)
-    vmem = pl.BlockSpec(memory_space=pltpu.VMEM)
     return pl.pallas_call(
         functools.partial(ending, cells),
         out_shape=(
@@ -974,7 +1026,7 @@
         out_specs=(hbm, smem),
         scratch_shapes=[pltpu.VMEM(source.shape, f32), dma((planes, RADIX))],
         compiler_params=pltpu.CompilerParams(vmem_limit_bytes=20 << 20),
-    )(slabs, sums, *back)
+    )(partial, tail, sums, final)
 
 
 def solution(mesh):

time: 58.1 us -> 57 us (0.981)
  Pallas kernels: 57.3 us -> 56.2 us
    pallas_call x1, Pallas kernels: 54.5 us -> 53.9 us  [body(): pl.pallas_call(functools.partial(kernel, groups, planes, CHUNKS, layers),...]
where the time goes in v5:
time: 57 us; the launch traced here: 56.8 us
  Pallas kernels  56.2 us (99%)
  between operations  0.65 us (1%)
    pallas_call x1, Pallas kernels, body(): pl.pallas_call(functools.partial(kernel, groups, planes, CHUNKS, layers),...  53.9 us
    pallas_call x1, Pallas kernels, body(): pl.pallas_call(functools.partial(ending, cells), out_shape=(jax.ShapeDtyp...  2.27 us

profile of v5, /device:TPU:1, one launch (start us, length us, event | category | flops | bytes accessed | tf_op | source)
XLA Modules:
  0.0 56.8 jit_solution(18002625288584297485)
XLA Ops:
  0.6 0.0 copy-start
  0.6 53.9 %shard_map.140 = (f32[2,4,256,256]{3,2,1,0:T(8,128)S(1)}, f32[4,2,2,16,256]{4,3,2,1,0:T(8,128)S(1)}, f32[16,2,128]{2,1,0:T(2,128)S(1)}) custom-call(f32[2,2,512,256]{3,2,1,0:T(8,128)} %source_hbm.1, s32[2,256]{1,0:T(2,128)} %ids_hbm.1, f32[16]{0:T(128)} %table_hbm.1, f32[2]{0:T(128)} %shift_hbm.1, f32[4,8,16,128]{3,2,1,0:T(8,128)} %constant.25.clone.mode_hbm, ...), custom_call_target="tpu_custom_call" | custom-call | tf_op jit(solution)/shard_map/pallas_call | solution.py:959
  54.6 0.0 copy-done
  54.6 2.3 %shard_map.141 = (f32[2,2,512,256]{3,2,1,0:T(8,128)}, f32[2]{0:T(128)}) custom-call(f32[2,4,256,256]{3,2,1,0:T(8,128)S(1)} %get-tuple-element.5.partial, f32[4,2,2,16,256]{4,3,2,1,0:T(8,128)S(1)} %get-tuple-element.6.tail, f32[16,2,128]{2,1,0:T(2,128)S(1)} %get-tuple-element.7.sums, bf16[4,256,96]{2,1,0:T(8,128)(2,1)S(1)} %copy-done), custom_call_target="tpu_custom_call" | custom-call | tf_op jit(solution)/shard_map/pallas_call | solution.py:1019
Async XLA Ops:
  0.6 53.9 %copy-start = (bf16[4,256,96]{2,1,0:T(8,128)(2,1)S(1)}, bf16[4,256,96]{2,1,0:T(8,128)(2,1)}, u32[]{:S(2)}) copy-start(bf16[4,256,96]{2,1,0:T(8,128)(2,1)} %constant.24.clone.table) | copy-start | bytes 589828

commit v6 on v5

--- a/solution.py
+++ b/solution.py
@@ -324,7 +324,9 @@
 
     pieces = [(ids_hbm, ids), (table_hbm, table), (shift_hbm, shift)]
     pieces += [(source_hbm.at[:, 0], source.at[:, 0])]
-    for residue in range(RADIX):
+    across = jnp.where(side < RADIX // 2, RADIX // 2, 0)
+    for step in range(RADIX):
+        residue = lax.rem(across + step, RADIX)
         pieces += [(fwd_hi_hbm.at[residue], fwd_hi.at[residue])]
         pieces += [(fwd_lo_hbm.at[residue], fwd_lo.at[residue])]
     pieces += [(source_hbm.at[:, plane], source.at[:, plane]) for plane in range(1, planes)]
@@ -336,7 +338,8 @@
         pltpu.make_async_copy(src, dst, load_sem.at[index])
         for index, (src, dst) in enumerate(pieces)
     ]
-    for load in loads[:later]:
+    first = 4 + RADIX
+    for load in loads[:first]:
         load.start()
 
     def remote(src, dst, send, recv, target):
@@ -478,14 +481,15 @@
 
     for load in loads[:3]:
         load.wait()
+    for load in loads[first:later]:
+        load.start()
     found = jnp.zeros((planes, length_y), jnp.float32)
     for layer in range(layers):
         found = found + jnp.where(ids[...] == layer, table[layer], 0.0)
     cond_own[...] = found
     cond_team[side] = found
 
-    def forward(plane):
-        loads[3 if plane == 0 else 3 + 2 * RADIX + plane].wait()
+    def forward(plane, order, act):
         parts = [
             (
                 source[0, plane, q * count : (q + 1) * count, :],
@@ -493,10 +497,10 @@
             )
             for q in range(RADIX)
         ]
-        for residue in range(RADIX):
+        for step, residue in enumerate(order):
             if plane == 0:
-                loads[4 + 2 * residue].wait()
-                loads[5 + 2 * residue].wait()
+                loads[4 + 2 * step].wait()
+                loads[5 + 2 * step].wait()
             mixed = combine(parts, [-residue * q for q in range(RADIX)])
             right = split(jnp.concatenate(mixed, axis=0))
             values = dot3((fwd_hi[residue], fwd_lo[residue]), right)
@@ -504,16 +508,33 @@
                 for part in range(2):
                     start = part * count + chunk * modes
                     spectra[residue, chunk, plane, part] = values[start : start + modes]
+            act(step, residue)
 
     ends = jnp.where((team > 0) & (team < teams - 1), 0, 1)
     pl.semaphore_wait(barrier, RADIX + 1 - ends)
     for offset in range(1, RADIX):
         cond_copy(offset).start()
-    forward(0)
-    for offset in (2, 3, 1):
-        in_piece(0, offset, 0).start()
+    loads[3].wait()
+
+    def send_piece(step, residue):
+        if step < RADIX // 2:
+            in_piece(0, lax.rem(residue + RADIX - side, RADIX), 0).start()
+
+    halves_of = [list(range(RADIX // 2)), list(range(RADIX // 2, RADIX))]
+
+    @pl.when(side < RADIX // 2)
+    def _():
+        forward(0, halves_of[1] + halves_of[0], send_piece)
+
+    @pl.when(side >= RADIX // 2)
+    def _():
+        forward(0, halves_of[0] + halves_of[1], send_piece)
+
+    near = lax.rem(side + 1 - 2 * lax.rem(side, 2) + RADIX - side, RADIX)
+    in_piece(0, near, 0).start()
     for plane in range(1, planes):
-        forward(plane)
+        loads[3 + 2 * RADIX + plane].wait()
+        forward(plane, range(RADIX), lambda step, residue: None)
         for offset in (2, 3, 1):
             in_piece(0, offset, plane).start()
 
@@ -533,7 +554,6 @@
             in_copy(chunk, offset).start()
         return carry
 
-    lax.fori_loop(1, 2, send_in, 0)
     for offset in range(1, RADIX):
         cond_copy(offset).wait()
     total = jnp.zeros((1, length_y), jnp.float32)
@@ -554,7 +574,7 @@
     def _():
         edge_copy(1).start()
 
-    lax.fori_loop(2, chunks - 3, send_in, 0)
+    lax.fori_loop(1, chunks - 4, send_in, 0)
 
 
     @pl.when(team > 0)
@@ -593,7 +613,7 @@
     row_lane = lax.broadcasted_iota(jnp.int32, (8, length_y), 1)
     last = length_y - 1
 
-    lax.fori_loop(chunks - 3, chunks, send_in, 0)
+    lax.fori_loop(chunks - 4, chunks, send_in, 0)
 
     def keep(chunk, carry):
         forcing[chunk, rows(side)] = spectra[side, chunk]

time: 57 us -> 56.6 us (level)
  no operation moved by 1% of the time
where the time goes in v6:
time: 56.6 us; the launch traced here: 56.4 us
  Pallas kernels  55.8 us (99%)
  between operations  0.65 us (1%)
    pallas_call x1, Pallas kernels, body(): pl.pallas_call(functools.partial(kernel, groups, planes, CHUNKS, layers),...  53.5 us
    pallas_call x1, Pallas kernels, body(): pl.pallas_call(functools.partial(ending, cells), out_shape=(jax.ShapeDtyp...  2.28 us

profile of v6, /device:TPU:1, one launch (start us, length us, event | category | flops | bytes accessed | tf_op | source)
XLA Modules:
  0.0 56.4 jit_solution(15500614751272434117)
XLA Ops:
  0.6 0.0 copy-start
  0.6 53.5 %shard_map.140 = (f32[2,4,256,256]{3,2,1,0:T(8,128)S(1)}, f32[4,2,2,16,256]{4,3,2,1,0:T(8,128)S(1)}, f32[16,2,128]{2,1,0:T(2,128)S(1)}) custom-call(f32[2,2,512,256]{3,2,1,0:T(8,128)} %source_hbm.1, s32[2,256]{1,0:T(2,128)} %ids_hbm.1, f32[16]{0:T(128)} %table_hbm.1, f32[2]{0:T(128)} %shift_hbm.1, f32[4,8,16,128]{3,2,1,0:T(8,128)} %constant.25.clone.mode_hbm, ...), custom_call_target="tpu_custom_call" | custom-call | tf_op jit(solution)/shard_map/pallas_call | solution.py:979
  54.1 0.0 copy-done
  54.1 2.3 %shard_map.141 = (f32[2,2,512,256]{3,2,1,0:T(8,128)}, f32[2]{0:T(128)}) custom-call(f32[2,4,256,256]{3,2,1,0:T(8,128)S(1)} %get-tuple-element.5.partial, f32[4,2,2,16,256]{4,3,2,1,0:T(8,128)S(1)} %get-tuple-element.6.tail, f32[16,2,128]{2,1,0:T(2,128)S(1)} %get-tuple-element.7.sums, bf16[4,256,96]{2,1,0:T(8,128)(2,1)S(1)} %copy-done), custom_call_target="tpu_custom_call" | custom-call | tf_op jit(solution)/shard_map/pallas_call | solution.py:1039
Async XLA Ops:
  0.6 53.5 %copy-start = (bf16[4,256,96]{2,1,0:T(8,128)(2,1)S(1)}, bf16[4,256,96]{2,1,0:T(8,128)(2,1)}, u32[]{:S(2)}) copy-start(bf16[4,256,96]{2,1,0:T(8,128)(2,1)} %constant.24.clone.table) | copy-start | bytes 589828

commit v7 on v6

--- a/solution.py
+++ b/solution.py
@@ -699,16 +699,19 @@
         put(rest_out, choose(even, ends[2:], ends[:2]), turn_id, chunk)
 
     def relay(turn_id, chunk):
-        pair_copy(turn_id, chunk).wait_recv()
-
         @pl.when(inner)
         def _():
+            pair_copy(turn_id, chunk).wait_recv()
             more = times(pair(lines, chunk, 1), pair(pair_in, turn_id, chunk))
             put(comb_out, plus(pair(rest_out, turn_id, chunk), more), turn_id, chunk)
             comb_copy(turn_id, chunk, 1).start()
             comb_copy(turn_id, chunk, 0).start()
 
     def solve(turn_id, chunk):
+        @pl.when(jnp.logical_not(inner))
+        def _():
+            pair_copy(turn_id, chunk).wait_recv()
+
         comb_copy(turn_id, chunk, 0).wait_recv()
         near = pair(pair_in, turn_id, chunk)
         wide = pair(comb_in, turn_id, chunk)

time: 56.6 us -> 56.2 us (level)
  Pallas kernels: 55.8 us -> 55.2 us
where the time goes in v7:
time: 56.2 us; the launch traced here: 55.9 us
  Pallas kernels  55.2 us (98%)
  between operations  0.65 us (1%)
    pallas_call x1, Pallas kernels, body(): pl.pallas_call(functools.partial(kernel, groups, planes, CHUNKS, layers),...  52.9 us
    pallas_call x1, Pallas kernels, body(): pl.pallas_call(functools.partial(ending, cells), out_shape=(jax.ShapeDtyp...  2.28 us

profile of v7, /device:TPU:1, one launch (start us, length us, event | category | flops | bytes accessed | tf_op | source)
XLA Modules:
  0.0 55.9 jit_solution(16423813375086985078)
XLA Ops:
  0.6 0.0 copy-start
  0.6 52.9 %shard_map.140 = (f32[2,4,256,256]{3,2,1,0:T(8,128)S(1)}, f32[4,2,2,16,256]{4,3,2,1,0:T(8,128)S(1)}, f32[16,2,128]{2,1,0:T(2,128)S(1)}) custom-call(f32[2,2,512,256]{3,2,1,0:T(8,128)} %source_hbm.1, s32[2,256]{1,0:T(2,128)} %ids_hbm.1, f32[16]{0:T(128)} %table_hbm.1, f32[2]{0:T(128)} %shift_hbm.1, f32[4,8,16,128]{3,2,1,0:T(8,128)} %constant.25.clone.mode_hbm, ...), custom_call_target="tpu_custom_call" | custom-call | tf_op jit(solution)/shard_map/pallas_call | solution.py:982
  53.6 0.0 copy-done
  53.6 2.3 %shard_map.141 = (f32[2,2,512,256]{3,2,1,0:T(8,128)}, f32[2]{0:T(128)}) custom-call(f32[2,4,256,256]{3,2,1,0:T(8,128)S(1)} %get-tuple-element.5.partial, f32[4,2,2,16,256]{4,3,2,1,0:T(8,128)S(1)} %get-tuple-element.6.tail, f32[16,2,128]{2,1,0:T(2,128)S(1)} %get-tuple-element.7.sums, bf16[4,256,96]{2,1,0:T(8,128)(2,1)S(1)} %copy-done), custom_call_target="tpu_custom_call" | custom-call | tf_op jit(solution)/shard_map/pallas_call | solution.py:1042
Async XLA Ops:
  0.6 53.0 %copy-start = (bf16[4,256,96]{2,1,0:T(8,128)(2,1)S(1)}, bf16[4,256,96]{2,1,0:T(8,128)(2,1)}, u32[]{:S(2)}) copy-start(bf16[4,256,96]{2,1,0:T(8,128)(2,1)} %constant.24.clone.table) | copy-start | bytes 589828
